TPU v7x, 32 devices: a whole 2x2x4 slice. The times are simulated.
32 devices in a mesh: dp: 8 (over z, y), tensor: 4 (over x, core).
Axes of the slice: x: 2, y: 2, z: 4, core: 2. Of those that a mesh axis runs over, the one named last changes fastest.
Arguments:
- tokens: bfloat16 [4096, 2048], P(('dp', 'tensor')), may hold values from -6 to 6
- lengths: int32 [8, 4], P('dp'), may hold values from 0 to 512, as said below
- w_query: bfloat16 [2048, 2048], P(None, 'tensor'), may hold values from -0.125 to 0.125
- w_key: bfloat16 [2048, 2048], P(None, 'tensor'), may hold values from -0.125 to 0.125
- w_value: bfloat16 [2048, 2048], P(None, 'tensor'), may hold values from -0.125 to 0.125
- w_out: bfloat16 [2048, 2048], P('tensor'), may hold values from -0.125 to 0.125
- w_gate: bfloat16 [2048, 8192], P(None, 'tensor'), may hold values from -0.125 to 0.125
- w_up: bfloat16 [2048, 8192], P(None, 'tensor'), may hold values from -0.125 to 0.125
- w_down: bfloat16 [8192, 2048], P('tensor'), may hold values from -0.0625 to 0.0625
- gain_query: float32 [2048], P('tensor'), may hold values from 0.1 to 1.9
- gain_key: float32 [2048], P('tensor'), may hold values from 0.1 to 1.9
- gain_attn: float32 [2048], replicated, may hold values from 0.1 to 1.9
- gain_mlp: float32 [2048], replicated, may hold values from 0.1 to 1.9
- cotangent: bfloat16 [4096, 2048], P(('dp', 'tensor')), may hold values from -6 to 6
Outputs:
- output: bfloat16 [4096, 2048], P(('dp', 'tensor'))
- grad_tokens: bfloat16 [4096, 2048], P(('dp', 'tensor'))
- grad_w_query: float32 [2048, 2048], P('dp', 'tensor')
- grad_w_key: float32 [2048, 2048], P('dp', 'tensor')
- grad_w_value: float32 [2048, 2048], P('dp', 'tensor')
- grad_w_out: float32 [2048, 2048], P('tensor', 'dp')
- grad_w_gate: float32 [2048, 8192], P('dp', 'tensor')
- grad_w_up: float32 [2048, 8192], P('dp', 'tensor')
- grad_w_down: float32 [8192, 2048], P('tensor', 'dp')
- grad_gain_query: float32 [2048], P('tensor')
- grad_gain_key: float32 [2048], P('tensor')
- grad_gain_attn: float32 [2048], replicated
- grad_gain_mlp: float32 [2048], replicated
Inputs may be any that keep to these rules, and one draw needn't show every extreme that they name: Each row lists the lengths of its sequences in order, then zeros; every nonzero length is 128 or more and they sum to 512; row 0 holds one sequence of 512 tokens.
All inputs are finite; a program needn't handle non-finite values.
Results may differ from a plain program's by a relative error of at most 0.023.
Values may be sent and summed in bfloat16 or wider, within the bound.
A program may use at most 256 MiB of HBM per device.

v0:
```python
import math

import jax
import jax.numpy as jnp
from jax import lax
from jax.sharding import PartitionSpec as P

HD = 128
ROW_LEN = 512


EPS = 1e-06
THETA = 500000.0


def rotate(values, offsets, rot_sign):
    half_width = values.shape[-1] // 2
    frequency = jnp.exp(
        jnp.arange(half_width, dtype=jnp.float32) * (-2.0 * math.log(THETA) / values.shape[-1])
    )
    angles = offsets.astype(jnp.float32)[..., None, None] * frequency
    cosines = jnp.cos(angles)
    sine_part = rot_sign * jnp.sin(angles)
    first_half = values[..., :half_width]
    second_half = values[..., half_width:]
    return jnp.concatenate(
        [
            first_half * cosines - second_half * sine_part,
            second_half * cosines + first_half * sine_part,
        ],
        axis=-1,
    )


def row_layout(lengths_row):
    seq_ends = jnp.cumsum(lengths_row)
    position = jnp.arange(ROW_LEN, dtype=jnp.int32)
    passed = (position[:, None] >= seq_ends[None, :]).astype(jnp.int32)
    segment = jnp.sum(passed, axis=1)
    seq_start = jnp.sum(passed * lengths_row[None, :], axis=1)
    return (segment, position - seq_start)


def allowed_mask(segment):
    position = jnp.arange(segment.shape[0], dtype=jnp.int32)
    return (segment[:, None] == segment[None, :]) & (position[None, :] <= position[:, None])


def times_t(left_mat, right_mat):
    return lax.dot_general(
        left_mat, right_mat, (((1,), (1,)), ((), ())), preferred_element_type=jnp.float32
    )


def t_times(left_mat, right_mat):
    return lax.dot_general(
        left_mat, right_mat, (((0,), (0,)), ((), ())), preferred_element_type=jnp.float32
    )


def masked_scores(queries_low, keys_low, segment):
    scale_factor = 1.0 / math.sqrt(queries_low.shape[-1])
    scores = (
        jnp.einsum("qhd,khd->hqk", queries_low, keys_low, preferred_element_type=jnp.float32)
        * scale_factor
    )
    return jnp.where(allowed_mask(segment)[None], scores, -1e30)


def attend(block_item):
    queries_low, keys_low, values_low, segment = block_item
    scores = masked_scores(queries_low, keys_low, segment)
    row_max = jnp.max(scores, axis=-1, keepdims=True)
    shifted = jnp.exp(scores - row_max)
    row_total = jnp.sum(shifted, axis=-1, keepdims=True)
    attn_weights = (shifted / row_total).astype(jnp.bfloat16)
    mixed = jnp.einsum("hqk,khd->qhd", attn_weights, values_low, preferred_element_type=jnp.float32)
    return (mixed.astype(jnp.bfloat16), (row_max + jnp.log(row_total))[..., 0])


def attend_back(block_item):
    queries_low, keys_low, values_low, segment, log_total, grad_mixed = block_item
    scale_factor = 1.0 / math.sqrt(queries_low.shape[-1])
    scores = masked_scores(queries_low, keys_low, segment)
    attn_weights = jnp.exp(scores - log_total[..., None])
    grad_weights = jnp.einsum(
        "qhd,khd->hqk", grad_mixed, values_low, preferred_element_type=jnp.float32
    )
    row_dots = jnp.sum(attn_weights * grad_weights, axis=-1, keepdims=True)
    grad_scores = (attn_weights * (grad_weights - row_dots)).astype(jnp.bfloat16)
    grad_queries = scale_factor * jnp.einsum(
        "hqk,khd->qhd", grad_scores, keys_low, preferred_element_type=jnp.float32
    )
    grad_keys = scale_factor * jnp.einsum(
        "hqk,qhd->khd", grad_scores, queries_low, preferred_element_type=jnp.float32
    )
    grad_values = jnp.einsum(
        "hqk,qhd->khd",
        attn_weights.astype(jnp.bfloat16),
        grad_mixed,
        preferred_element_type=jnp.float32,
    )
    return (grad_queries, grad_keys, grad_values.astype(jnp.bfloat16))


def post_norm_back(grad_in, unit_rows, inv_scale, gain_vec):
    scaled = grad_in * gain_vec
    mean_dots = jnp.mean(scaled * unit_rows, axis=-1, keepdims=True)
    return (inv_scale * (scaled - unit_rows * mean_dots), jnp.sum(grad_in * unit_rows, axis=0))


def body(
    tokens,
    lengths,
    w_query,
    w_key,
    w_value,
    w_out,
    w_gate,
    w_up,
    w_down,
    gain_query,
    gain_key,
    gain_attn,
    gain_mlp,
    cotangent,
):
    rows_dev = lengths.shape[0]
    model_width = w_query.shape[0]
    local_width = w_query.shape[1]
    head_count = local_width // HD
    gathered = lax.all_gather(tokens, "tensor", axis=0, tiled=True)
    row_count = gathered.shape[0]
    segment, offsets = jax.vmap(row_layout)(lengths)
    queries = jnp.dot(gathered, w_query, preferred_element_type=jnp.float32)
    keys_raw = jnp.dot(gathered, w_key, preferred_element_type=jnp.float32)
    values_low = jnp.dot(gathered, w_value, preferred_element_type=jnp.float32).astype(jnp.bfloat16)
    q_total, k_total = lax.psum(
        (jnp.sum(queries * queries, axis=1), jnp.sum(keys_raw * keys_raw, axis=1)), "tensor"
    )
    q_inv = lax.rsqrt(q_total / model_width + EPS)[:, None]
    k_inv = lax.rsqrt(k_total / model_width + EPS)[:, None]
    q_unit = queries * q_inv
    k_unit = keys_raw * k_inv

    def to_heads(values):
        return values.reshape(rows_dev, ROW_LEN, head_count, HD)

    queries_low = rotate(to_heads(q_unit * gain_query), offsets, 1.0).astype(jnp.bfloat16)
    keys_low = rotate(to_heads(k_unit * gain_key), offsets, 1.0).astype(jnp.bfloat16)
    values_heads = to_heads(values_low)
    mixed_heads, log_total = lax.map(attend, (queries_low, keys_low, values_heads, segment))
    mixed_low = mixed_heads.reshape(row_count, local_width)
    attn_out = lax.psum_scatter(
        jnp.dot(mixed_low, w_out, preferred_element_type=jnp.float32).astype(jnp.bfloat16),
        "tensor",
        scatter_dimension=0,
        tiled=True,
    ).astype(jnp.float32)
    a_inv = lax.rsqrt(jnp.mean(attn_out * attn_out, axis=1, keepdims=True) + EPS)
    a_unit = attn_out * a_inv
    hidden = tokens.astype(jnp.float32) + a_unit * gain_attn
    hidden_all = lax.all_gather(hidden.astype(jnp.bfloat16), "tensor", axis=0, tiled=True)
    gate_acts = jnp.dot(hidden_all, w_gate, preferred_element_type=jnp.float32)
    up_acts = jnp.dot(hidden_all, w_up, preferred_element_type=jnp.float32)
    gate_sigmoid = jax.nn.sigmoid(gate_acts)
    inner_low = (gate_acts * gate_sigmoid * up_acts).astype(jnp.bfloat16)
    mlp_out = lax.psum_scatter(
        jnp.dot(inner_low, w_down, preferred_element_type=jnp.float32).astype(jnp.bfloat16),
        "tensor",
        scatter_dimension=0,
        tiled=True,
    ).astype(jnp.float32)
    f_inv = lax.rsqrt(jnp.mean(mlp_out * mlp_out, axis=1, keepdims=True) + EPS)
    f_unit = mlp_out * f_inv
    output = (hidden + f_unit * gain_mlp).astype(jnp.bfloat16)
    grad_output = cotangent.astype(jnp.float32)
    grad_mlp, grad_gain_mlp_part = post_norm_back(grad_output, f_unit, f_inv, gain_mlp)
    mlp_grad_all = lax.all_gather(grad_mlp.astype(jnp.bfloat16), "tensor", axis=0, tiled=True)
    grad_w_down = t_times(inner_low, mlp_grad_all)
    grad_inner = times_t(mlp_grad_all, w_down)
    grad_gate_low = (
        grad_inner * up_acts * gate_sigmoid * (1.0 + gate_acts * (1.0 - gate_sigmoid))
    ).astype(jnp.bfloat16)
    grad_up_low = (grad_inner * gate_acts * gate_sigmoid).astype(jnp.bfloat16)
    grad_w_gate = t_times(hidden_all, grad_gate_low)
    grad_w_up = t_times(hidden_all, grad_up_low)
    grad_hidden = grad_output + lax.psum_scatter(
        (times_t(grad_gate_low, w_gate) + times_t(grad_up_low, w_up)).astype(jnp.bfloat16),
        "tensor",
        scatter_dimension=0,
        tiled=True,
    ).astype(jnp.float32)
    grad_attn, grad_gain_attn_part = post_norm_back(grad_hidden, a_unit, a_inv, gain_attn)
    attn_grad_all = lax.all_gather(grad_attn.astype(jnp.bfloat16), "tensor", axis=0, tiled=True)
    grad_w_out = t_times(mixed_low, attn_grad_all)
    grad_mixed = times_t(attn_grad_all, w_out).astype(jnp.bfloat16)
    grad_q_rot, grad_k_rot, grad_values_low = lax.map(
        attend_back, (queries_low, keys_low, values_heads, segment, log_total, to_heads(grad_mixed))
    )
    grad_q_norm = rotate(grad_q_rot, offsets, -1.0).reshape(row_count, local_width)
    grad_k_norm = rotate(grad_k_rot, offsets, -1.0).reshape(row_count, local_width)
    grad_gain_query_part = jnp.sum(grad_q_norm * q_unit, axis=0)
    grad_gain_key_part = jnp.sum(grad_k_norm * k_unit, axis=0)
    q_scaled = grad_q_norm * gain_query
    k_scaled = grad_k_norm * gain_key
    q_dots, k_dots = lax.psum(
        (jnp.sum(q_scaled * q_unit, axis=1), jnp.sum(k_scaled * k_unit, axis=1)), "tensor"
    )
    grad_queries_low = (q_inv * (q_scaled - q_unit * (q_dots / model_width)[:, None])).astype(
        jnp.bfloat16
    )
    grad_keys_low = (k_inv * (k_scaled - k_unit * (k_dots / model_width)[:, None])).astype(
        jnp.bfloat16
    )
    grad_values_flat = grad_values_low.reshape(row_count, local_width)
    grad_w_query = t_times(gathered, grad_queries_low)
    grad_w_key = t_times(gathered, grad_keys_low)
    grad_w_value = t_times(gathered, grad_values_flat)
    grad_tokens = (
        grad_hidden
        + lax.psum_scatter(
            (
                times_t(grad_queries_low, w_query)
                + times_t(grad_keys_low, w_key)
                + times_t(grad_values_flat, w_value)
            ).astype(jnp.bfloat16),
            "tensor",
            scatter_dimension=0,
            tiled=True,
        ).astype(jnp.float32)
    ).astype(jnp.bfloat16)
    tensor_start = lax.axis_index("tensor") * local_width
    zero_row = jnp.zeros((model_width,), jnp.float32)
    q_full = lax.dynamic_update_slice(zero_row, grad_gain_query_part, (tensor_start,))
    k_full = lax.dynamic_update_slice(zero_row, grad_gain_key_part, (tensor_start,))
    gain_stack = jnp.stack([q_full, k_full, grad_gain_attn_part, grad_gain_mlp_part])
    gain_total = lax.psum(gain_stack, ("dp", "tensor"))
    grad_gain_query = lax.dynamic_slice(gain_total[0], (tensor_start,), (local_width,))
    grad_gain_key = lax.dynamic_slice(gain_total[1], (tensor_start,), (local_width,))
    summed = (
        lax.psum_scatter(
            grad_w_query.astype(jnp.bfloat16), "dp", scatter_dimension=0, tiled=True
        ).astype(jnp.float32),
        lax.psum_scatter(
            grad_w_key.astype(jnp.bfloat16), "dp", scatter_dimension=0, tiled=True
        ).astype(jnp.float32),
        lax.psum_scatter(
            grad_w_value.astype(jnp.bfloat16), "dp", scatter_dimension=0, tiled=True
        ).astype(jnp.float32),
        lax.psum_scatter(
            grad_w_out.astype(jnp.bfloat16), "dp", scatter_dimension=1, tiled=True
        ).astype(jnp.float32),
        lax.psum_scatter(
            grad_w_gate.astype(jnp.bfloat16), "dp", scatter_dimension=0, tiled=True
        ).astype(jnp.float32),
        lax.psum_scatter(
            grad_w_up.astype(jnp.bfloat16), "dp", scatter_dimension=0, tiled=True
        ).astype(jnp.float32),
        lax.psum_scatter(
            grad_w_down.astype(jnp.bfloat16), "dp", scatter_dimension=1, tiled=True
        ).astype(jnp.float32),
    )
    return (
        output,
        grad_tokens,
        summed[0],
        summed[1],
        summed[2],
        summed[3],
        summed[4],
        summed[5],
        summed[6],
        grad_gain_query,
        grad_gain_key,
        gain_total[2],
        gain_total[3],
    )


def solution(mesh):
    placed = (
        P(("dp", "tensor"), None),
        P("dp", None),
        P(None, "tensor"),
        P(None, "tensor"),
        P(None, "tensor"),
        P("tensor", None),
        P(None, "tensor"),
        P(None, "tensor"),
        P("tensor", None),
        P("tensor"),
        P("tensor"),
        P(),
        P(),
        P(("dp", "tensor"), None),
    )
    return jax.shard_map(
        body,
        mesh=mesh,
        in_specs=placed,
        out_specs=(
            P(("dp", "tensor"), None),
            P(("dp", "tensor"), None),
            P("dp", "tensor"),
            P("dp", "tensor"),
            P("dp", "tensor"),
            P("tensor", "dp"),
            P("dp", "tensor"),
            P("dp", "tensor"),
            P("tensor", "dp"),
            P("tensor"),
            P("tensor"),
            P(),
            P(),
        ),
        check_vma=False,
    )
```

profile of v0, /device:TPU:0, one launch (start us, length us, event | category | flops | bytes accessed | tf_op | source)
XLA Modules:
  0.0 1118.6 jit_solution(15427189430564919261)
XLA Ops:
  10.5 1.8 broadcast_multiply_fusion
  12.3 22.6 %all-gather.5.cloned.1.call-done = bf16[512,2048]{1,0:T(8,128)(2,1)} async-done(((bf16[128,2048]{1,0:T(8,128)(2,1)}), bf16[512,2048]{1,0:T(8,128)(2,1)}) %all-gather.5.cloned.1.call-update) | async-done | bytes 2097168 | tf_op jit(solution)/shard_map/all_gather | solution.py:132
  34.9 4.0 multiply_reduce_fusion.4
  38.9 2.3 multiply_reduce_fusion.3
  41.2 5.9 all-reduce.1
  47.1 1.4 multiply_multiply_fusion.1
  49.9 1.3 copy.75
  51.2 1.4 multiply_multiply_fusion
  55.3 2.8 fusion.41
  58.2 1.4 fusion.51
  60.3 2.5 copy-done.19
  66.5 2.6 convolution_convert_fusion.8
  69.2 32.6 %reduce-scatter.12.cloned.1.call-done = bf16[128,2048]{1,0:T(8,128)(2,1)} async-done(((bf16[512,2048]{1,0:T(8,128)(2,1)}), bf16[128,2048]{1,0:T(8,128)(2,1)}) %reduce-scatter.12.cloned.1.call-update) | async-done | bytes 524304 | tf_op jit(solution)/shard_map/reduce_scatter | solution.py:154
  103.0 2.1 fusion.40
  105.4 22.5 %all-gather.7.cloned.1.call-done = bf16[512,2048]{1,0:T(8,128)(2,1)} async-done(((bf16[128,2048]{1,0:T(8,128)(2,1)}), bf16[512,2048]{1,0:T(8,128)(2,1)}) %all-gather.7.cloned.1.call-update) | async-done | bytes 2097168 | tf_op jit(solution)/shard_map/all_gather | solution.py:163
  127.9 8.5 fusion.52
  136.4 11.7 %multiply_convert_fusion.3 = (bf16[512,2048]{1,0:T(8,128)(2,1)S(1)}, f32[512,2048]{1,0:T(8,128)}) fusion(f32[512,2048]{1,0:T(8,128)S(1)} %fusion.52, bf16[512,2048]{1,0:T(8,128)(2,1)S(1)} %copy-done.40, bf16[2048,2048]{1,0:T(8,128)(2,1)} %param.21), kind=kOutput, calls=%fused_computation.10 | convolution fusion | flops 4301258752 | bytes 20971520 | tf_op jit(solution)/shard_map/dot_general | solution.py:165
  148.1 1.4 copy-done.43
  149.5 5.7 convolution_convert_fusion.7
  155.3 31.5 %reduce-scatter.14.cloned.1.call-done = bf16[128,2048]{1,0:T(8,128)(2,1)} async-done(((bf16[512,2048]{1,0:T(8,128)(2,1)}), bf16[128,2048]{1,0:T(8,128)(2,1)}) %reduce-scatter.14.cloned.1.call-update) | async-done | bytes 524304 | tf_op jit(solution)/shard_map/reduce_scatter | solution.py:168
  188.1 1.5 fusion.36
  189.5 2.2 fusion.24
  192.2 22.3 %all-gather.9.cloned.1.call-done = bf16[512,2048]{1,0:T(8,128)(2,1)} async-done(((bf16[128,2048]{1,0:T(8,128)(2,1)}), bf16[512,2048]{1,0:T(8,128)(2,1)}) %all-gather.9.cloned.1.call-update) | async-done | bytes 2097168 | tf_op jit(solution)/shard_map/all_gather | solution.py:179
  214.5 11.9 %multiply_convert_fusion.1 = (bf16[512,2048]{1,0:T(8,128)(2,1)S(1)}, bf16[512,2048]{1,0:T(8,128)(2,1)S(1)}) fusion(f32[512,2048]{1,0:T(8,128)} %copy-done.42, f32[512,2048]{1,0:T(8,128)} %get-tuple-element.138, bf16[512,2048]{1,0:T(8,128)(2,1)} %all-gather.9.cloned.1.call-done, bf16[2048,2048]{1,0:T(8,128)(2,1)} %param.22), kind=kOutput, calls=%fused_computation.8 | convolution fusion | flops 4308598784 | bytes 23068672 | tf_op jit(solution)/shard_map/dot_general | solution.py:50
  226.4 8.5 fusion.53
  234.9 9.2 add_convert_fusion.1
  244.2 31.6 %reduce-scatter.16.cloned.1.call-done = bf16[128,2048]{1,0:T(8,128)(2,1)} async-done(((bf16[512,2048]{1,0:T(8,128)(2,1)}), bf16[128,2048]{1,0:T(8,128)(2,1)}) %reduce-scatter.16.cloned.1.call-update) | async-done | bytes 524304 | tf_op jit(solution)/shard_map/reduce_scatter | solution.py:188
  275.7 1.5 fusion.30
  277.3 2.9 fusion.29
  280.5 22.5 %all-gather.11.cloned.1.call-done = bf16[512,2048]{1,0:T(8,128)(2,1)} async-done(((bf16[128,2048]{1,0:T(8,128)(2,1)}), bf16[512,2048]{1,0:T(8,128)(2,1)}) %all-gather.11.cloned.1.call-update) | async-done | bytes 2097168 | tf_op jit(solution)/shard_map/all_gather | solution.py:195
  303.0 3.6 convolution_convert_fusion.9
  311.2 2.0 multiply_subtract_fusion
  314.5 2.6 copy.56
  317.1 2.0 fusion.38
  320.6 2.5 copy.60
  323.1 1.9 fusion.37
  325.0 5.9 all-reduce
  330.9 1.9 multiply_convert_fusion.5
  333.1 2.6 fusion.2
  335.7 1.9 multiply_convert_fusion.4
  338.5 2.6 fusion.3
  341.1 3.3 fusion.18
  345.3 2.6 fusion.4
  348.2 4.3 convolution_convert_fusion.3
  356.1 2.6 add_convert_fusion
  358.8 10.0 convolution_convert_fusion.2
  369.1 10.1 convolution_convert_fusion.1
  379.3 10.0 convolution_convert_fusion
  389.5 40.7 %psum.39 = f32[4,2048]{1,0:T(4,128)S(1)} all-reduce(f32[4,2048]{1,0:T(4,128)S(1)} %pad_maximum_fusion.8), channel_id=1, replica_groups=mesh['dp'=8,'tensor'=4] {'dp','tensor'}, use_global_device_ids=true, to_apply=%region_33.34 | all-reduce | flops 8192 | bytes 65536 | tf_op jit(solution)/shard_map/psum | solution.py:238
  431.9 1.9 copy.62
  433.8 43.0 %reduce-scatter.22.cloned.1.call-done = bf16[256,512]{0,1:T(8,128)(2,1)} async-done(((bf16[2048,512]{0,1:T(8,128)(2,1)}), bf16[256,512]{0,1:T(8,128)(2,1)}) %reduce-scatter.22.cloned.1.call-update) | async-done | bytes 262160 | tf_op jit(solution)/shard_map/reduce_scatter | solution.py:245
  476.9 1.9 copy.63
  478.8 69.0 %reduce-scatter.24.cloned.1.call-done = bf16[256,512]{0,1:T(8,128)(2,1)} async-done(((bf16[2048,512]{0,1:T(8,128)(2,1)}), bf16[256,512]{0,1:T(8,128)(2,1)}) %reduce-scatter.24.cloned.1.call-update) | async-done | bytes 262160 | tf_op jit(solution)/shard_map/reduce_scatter | solution.py:248
  547.7 1.9 copy.64
  549.6 69.2 %reduce-scatter.26.cloned.1.call-done = bf16[512,256]{1,0:T(8,128)(2,1)} async-done(((bf16[512,2048]{1,0:T(8,128)(2,1)}), bf16[512,256]{1,0:T(8,128)(2,1)}) %reduce-scatter.26.cloned.1.call-update) | async-done | bytes 262160 | tf_op jit(solution)/shard_map/reduce_scatter | solution.py:251
  618.8 1.8 convert_element_type.215
  620.6 31.8 %reduce-scatter.18.cloned.1.call-done = bf16[128,2048]{1,0:T(8,128)(2,1)} async-done(((bf16[512,2048]{1,0:T(8,128)(2,1)}), bf16[128,2048]{1,0:T(8,128)(2,1)}) %reduce-scatter.18.cloned.1.call-update) | async-done | bytes 524304 | tf_op jit(solution)/shard_map/reduce_scatter | solution.py:222
  652.4 2.1 add_convert_fusion.2
  654.4 150.6 %reduce-scatter.28.cloned.1.call-done = bf16[256,2048]{1,0:T(8,128)(2,1)} async-done(((bf16[2048,2048]{1,0:T(8,128)(2,1)}), bf16[256,2048]{1,0:T(8,128)(2,1)}) %reduce-scatter.28.cloned.1.call-update) | async-done | bytes 1048592 | tf_op jit(solution)/shard_map/reduce_scatter | solution.py:254
  805.0 2.8 convert_element_type.217
  807.8 149.2 %reduce-scatter.30.cloned.1.call-done = bf16[256,2048]{1,0:T(8,128)(2,1)} async-done(((bf16[2048,2048]{1,0:T(8,128)(2,1)}), bf16[256,2048]{1,0:T(8,128)(2,1)}) %reduce-scatter.30.cloned.1.call-update) | async-done | bytes 1048592 | tf_op jit(solution)/shard_map/reduce_scatter | solution.py:257
  957.0 2.8 convert_element_type.219
  959.8 149.1 %reduce-scatter.32.cloned.1.call-done = bf16[2048,256]{1,0:T(8,128)(2,1)} async-done(((bf16[2048,2048]{1,0:T(8,128)(2,1)}), bf16[2048,256]{1,0:T(8,128)(2,1)}) %reduce-scatter.32.cloned.1.call-update) | async-done | bytes 1048592 | tf_op jit(solution)/shard_map/reduce_scatter | solution.py:260
  1108.9 2.7 convert_element_type.221
  (165 shorter events, 30.7 us)
Async XLA Ops:
  7.2 27.7 %copy-start = (bf16[2048,512]{1,0:T(8,128)(2,1)S(1)}, bf16[2048,512]{1,0:T(8,128)(2,1)}, u32[]{:S(2)}) copy-start(bf16[2048,512]{1,0:T(8,128)(2,1)} %param.16) | copy-start | bytes 6291460
  7.2 27.7 %all-gather.5.cloned.1.call-start = ((), (), s32[]{:S(2)}) async-start(), calls=%async_computation.11 | async-start | bytes 2621440 | tf_op jit(solution)/shard_map/all_gather | solution.py:132
  7.9 93.8 %reduce-scatter.12.cloned.1.call-start = ((), (), s32[]{:S(2)}) async-start(), calls=%async_computation.12 | async-start | bytes 2621440 | tf_op jit(solution)/shard_map/reduce_scatter | solution.py:154
  34.9 4.0 copy-start.24
  34.9 4.0 copy-start.35
  38.9 8.1 copy-start.32
  48.5 2.7 copy-start.33
  55.3 2.9 copy-start.26
  58.2 1.4 copy-start.7
  58.2 1.4 copy-start.9
  58.2 1.4 copy-start.11
  58.2 1.4 copy-start.13
  59.6 5.1 copy-start.1
  59.6 3.1 copy-start.19
  59.7 3.7 copy-start.36
  64.7 1.0 copy-start.28
  64.7 1.8 copy-start.34
  65.7 0.8 copy-start.41
  69.1 33.9 %copy-start.5 = (bf16[128,2048]{1,0:T(8,128)(2,1)S(1)}, bf16[128,2048]{1,0:T(8,128)(2,1)}, u32[]{:S(2)}) copy-start(bf16[128,2048]{1,0:T(8,128)(2,1)} %param.14) | copy-start | bytes 1572868
  69.1 33.9 %copy-start.30 = (f32[2048]{0:T(1024)S(1)}, f32[2048]{0:T(1024)}, u32[]{:S(2)}) copy-start(f32[2048]{0:T(1024)} %param.25) | copy-start | bytes 24580
  69.1 58.8 %all-gather.7.cloned.1.call-start = ((), (), s32[]{:S(2)}) async-start(), calls=%async_computation.13 | async-start | bytes 2621440 | tf_op jit(solution)/shard_map/all_gather | solution.py:163
  105.1 81.7 %reduce-scatter.14.cloned.1.call-start = ((), (), s32[]{:S(2)}) async-start(), calls=%async_computation.14 | async-start | bytes 2621440 | tf_op jit(solution)/shard_map/reduce_scatter | solution.py:168
  127.9 8.5 copy-start.40
  127.9 21.6 %slice-start = ((s8[8388608]{0:T(1024)(128)(4,1)}), s8[4194304]{0:T(1024)(128)(4,1)S(1)}, s32[]{:S(2)}) async-start(s8[8388608]{0:T(1024)(128)(4,1)} %bitcast.128), calls=%async_computation.26 | async-start | bytes 8388608
  136.4 11.7 %copy-start.42 = (f32[512,2048]{1,0:T(8,128)}, f32[512,2048]{1,0:T(8,128)S(1)}, u32[]{:S(2)}) copy-start(f32[512,2048]{1,0:T(8,128)S(1)} %fusion.52) | copy-start | bytes 12582916
  136.4 13.1 %slice-start.1 = ((s8[8388608]{0:T(1024)(128)(4,1)}), s8[4194304]{0:T(1024)(128)(4,1)S(1)}, s32[]{:S(2)}) async-start(s8[8388608]{0:T(1024)(128)(4,1)} %bitcast.128), calls=%async_computation.27 | async-start | bytes 8388608
  148.1 1.4 copy-start.43
  155.2 32.9 %copy-start.3 = (bf16[128,2048]{1,0:T(8,128)(2,1)S(1)}, bf16[128,2048]{1,0:T(8,128)(2,1)}, u32[]{:S(2)}) copy-start(bf16[128,2048]{1,0:T(8,128)(2,1)} %param.27) | copy-start | bytes 1572868
  155.2 32.9 %copy-start.31 = (f32[2048]{0:T(1024)S(1)}, f32[2048]{0:T(1024)}, u32[]{:S(2)}) copy-start(f32[2048]{0:T(1024)} %param.26) | copy-start | bytes 24580
  155.2 59.3 %all-gather.9.cloned.1.call-start = ((), (), s32[]{:S(2)}) async-start(), calls=%async_computation.15 | async-start | bytes 2621440 | tf_op jit(solution)/shard_map/all_gather | solution.py:179
  191.8 84.0 %reduce-scatter.16.cloned.1.call-start = ((), (), s32[]{:S(2)}) async-start(), calls=%async_computation.16 | async-start | bytes 2621440 | tf_op jit(solution)/shard_map/reduce_scatter | solution.py:188
  226.4 8.5 copy-start.45
  226.4 8.5 copy-start.44
  244.1 31.6 %copy-start.4 = (bf16[128,2048]{1,0:T(8,128)(2,1)S(1)}, bf16[128,2048]{1,0:T(8,128)(2,1)}, u32[]{:S(2)}) copy-start(bf16[128,2048]{1,0:T(8,128)(2,1)} %reduce-scatter.12.cloned.1.call-done) | copy-start | bytes 1572868
  244.1 58.8 %all-gather.11.cloned.1.call-start = ((), (), s32[]{:S(2)}) async-start(), calls=%async_computation.17 | async-start | bytes 2621440 | tf_op jit(solution)/shard_map/all_gather | solution.py:195
  280.2 151.7 %reduce-scatter.20.cloned.1.call-start = ((), (), s32[]{:S(2)}) async-start(), calls=%async_computation.19 | async-start | bytes 2359296 | tf_op jit(solution)/shard_map/reduce_scatter | solution.py:242
  280.5 26.2 %copy-start.29 = (bf16[512,512]{0,1:T(8,128)(2,1)S(1)}, bf16[512,512]{0,1:T(8,128)(2,1)}, u32[]{:S(2)}) copy-start(bf16[512,512]{0,1:T(8,128)(2,1)} %copy-done.28) | copy-start | bytes 1572868
  303.0 3.7 copy-start.2
  306.6 1.0 copy-start.21
  307.6 1.2 copy-start.12
  307.6 1.2 copy-start.14
  308.9 1.0 copy-start.8
  308.9 1.2 copy-start.10
  310.1 1.1 copy-start.27
  317.1 2.0 copy-start.15
  317.1 2.2 copy-start.16
  330.9 2.2 copy-start.37
  335.7 141.2 %reduce-scatter.22.cloned.1.call-start = ((), (), s32[]{:S(2)}) async-start(), calls=%async_computation.20 | async-start | bytes 2359296 | tf_op jit(solution)/shard_map/reduce_scatter | solution.py:245
  335.7 2.7 copy-start.38
  337.7 0.8 copy-start.17
  341.1 206.7 %reduce-scatter.24.cloned.1.call-start = ((), (), s32[]{:S(2)}) async-start(), calls=%async_computation.21 | async-start | bytes 2359296 | tf_op jit(solution)/shard_map/reduce_scatter | solution.py:248
  341.1 4.2 copy-start.39
  344.5 0.8 copy-start.22
  347.9 270.9 %reduce-scatter.26.cloned.1.call-start = ((), (), s32[]{:S(2)}) async-start(), calls=%async_computation.22 | async-start | bytes 2359296 | tf_op jit(solution)/shard_map/reduce_scatter | solution.py:251
  352.5 299.8 %reduce-scatter.18.cloned.1.call-start = ((), (), s32[]{:S(2)}) async-start(), calls=%async_computation.18 | async-start | bytes 2621440 | tf_op jit(solution)/shard_map/reduce_scatter | solution.py:222
  352.6 1.3 copy-start.18
  352.6 1.8 copy-start.25
  354.4 1.6 copy-start.20
  354.4 1.7 copy-start.23
  358.7 446.3 %reduce-scatter.28.cloned.1.call-start = ((), (), s32[]{:S(2)}) async-start(), calls=%async_computation.23 | async-start | bytes 9437184 | tf_op jit(solution)/shard_map/reduce_scatter | solution.py:254
  368.8 588.2 %reduce-scatter.30.cloned.1.call-start = ((), (), s32[]{:S(2)}) async-start(), calls=%async_computation.24 | async-start | bytes 9437184 | tf_op jit(solution)/shard_map/reduce_scatter | solution.py:257
  379.2 729.7 %reduce-scatter.32.cloned.1.call-start = ((), (), s32[]{:S(2)}) async-start(), calls=%async_computation.25 | async-start | bytes 9437184 | tf_op jit(solution)/shard_map/reduce_scatter | solution.py:260
  389.3 263.0 %copy-start.6 = (bf16[128,2048]{1,0:T(8,128)(2,1)S(1)}, bf16[128,2048]{1,0:T(8,128)(2,1)}, u32[]{:S(2)}) copy-start(bf16[128,2048]{1,0:T(8,128)(2,1)} %reduce-scatter.16.cloned.1.call-done) | copy-start | bytes 1572868
Sparse Core Ops, SparseCore 0:
  9.6 25.2 all-gather.4
  69.2 32.4 reduce-scatter.11
  105.3 22.5 all-gather.6
  155.3 31.4 reduce-scatter.13
  191.9 22.5 all-gather.8
  244.3 31.4 reduce-scatter.15
  280.4 22.5 all-gather.10
  335.8 69.3 reduce-scatter.19
  409.7 67.1 reduce-scatter.21
  480.7 67.0 reduce-scatter.23
  551.7 67.0 reduce-scatter.25
  621.9 30.3 reduce-scatter.17
  656.0 149.0 reduce-scatter.27
  808.9 148.0 reduce-scatter.29
  960.5 148.3 reduce-scatter.31
where the time goes:
time: 1130 us; the launch traced here: 1120 us
  waiting for transfers between devices  848 us (75%)
  matrix products  125 us (11%)
  blocking collectives  52.4 us (5%)
  other arithmetic  48.9 us (4%)
  local copies, waits for them, and re-layouts  26.8 us (2%)
  between operations  15 us (1%)
    reduce_scatter x1, waiting for transfers between devices, body(): lax.psum_scatter(grad_w_gate.astype(jnp.bfloat16), 'dp', scatter_dimensio...  151 us
    reduce_scatter x1, waiting for transfers between devices, body(): lax.psum_scatter(grad_w_up.astype(jnp.bfloat16), 'dp', scatter_dimension=...  149 us
    reduce_scatter x1, waiting for transfers between devices, body(): lax.psum_scatter(grad_w_down.astype(jnp.bfloat16), 'dp', scatter_dimensio...  149 us
    reduce_scatter x1, waiting for transfers between devices, body(): lax.psum_scatter(grad_w_out.astype(jnp.bfloat16), 'dp', scatter_dimension...  69.2 us
    reduce_scatter x1, waiting for transfers between devices, body(): lax.psum_scatter(grad_w_value.astype(jnp.bfloat16), 'dp', scatter_dimensi...  69 us
    reduce_scatter x1, waiting for transfers between devices, body(): lax.psum_scatter(grad_w_key.astype(jnp.bfloat16), 'dp', scatter_dimension...  43 us
    dot_general x7, matrix products, t_times(): lax.dot_general(left_mat, right_mat, (((0,), (0,)), ((), ())), preferred_...  42.3 us
    psum x1, blocking collectives, body(): gain_total = lax.psum(gain_stack, ('dp', 'tensor'))  40.7 us
  transfers between devices with their start and end apart: 15, of which 14 were waited for; matrix products, arithmetic and copies ran while one was open for 6% of the time, Pallas kernels for 0%

commit v1 on v0

--- a/solution.py
+++ b/solution.py
@@ -33,7 +33,10 @@
 
 
 def row_layout(lengths_row):
-    seq_ends = jnp.cumsum(lengths_row)
+    slots = jnp.arange(lengths_row.shape[0], dtype=jnp.int32)
+    seq_ends = jnp.sum(
+        jnp.where(slots[None, :] <= slots[:, None], lengths_row[None, :], 0), axis=1
+    )
     position = jnp.arange(ROW_LEN, dtype=jnp.int32)
     passed = (position[:, None] >= seq_ends[None, :]).astype(jnp.int32)
     segment = jnp.sum(passed, axis=1)
@@ -107,6 +110,62 @@
     scaled = grad_in * gain_vec
     mean_dots = jnp.mean(scaled * unit_rows, axis=-1, keepdims=True)
     return (inv_scale * (scaled - unit_rows * mean_dots), jnp.sum(grad_in * unit_rows, axis=0))
+
+
+OUTER = 4
+
+
+def swap(value, shift):
+    size = lax.axis_size("dp")
+    return lax.ppermute(value, "dp", [(d, d ^ shift) for d in range(size)])
+
+
+def pick(parts, index):
+    return lax.dynamic_index_in_dim(parts, index, 0, keepdims=False)
+
+
+def sum_inner(parts):
+    inner = parts.shape[0]
+    mine = lax.axis_index("dp") % inner
+    total = pick(parts, mine)
+    for k in range(1, inner):
+        sent = pick(parts, mine ^ k).astype(jnp.bfloat16)
+        total = total + swap(sent, k).astype(jnp.float32)
+    return total
+
+
+def trade_outer(parts, inner):
+    mine = lax.axis_index("dp") // inner
+    got = [(mine, pick(parts, mine))]
+    for k in range(1, OUTER):
+        got.append((mine ^ k, swap(pick(parts, mine ^ k), k * inner)))
+    return got
+
+
+def split_rows(grad, inner):
+    cols = grad.shape[1]
+    return grad.reshape(OUTER, inner, -1, cols).transpose(1, 0, 2, 3)
+
+
+def split_cols(grad, inner):
+    rows = grad.shape[0]
+    return grad.reshape(rows, OUTER, inner, -1).transpose(2, 1, 0, 3)
+
+
+def scatter_sum(parts, inner):
+    half = sum_inner(parts).astype(jnp.bfloat16)
+    got = trade_outer(half, inner)
+    return sum(g.astype(jnp.float32) for _, g in got)
+
+
+def scatter_join(parts, inner, axis):
+    half = sum_inner(parts).astype(jnp.bfloat16)
+    got = trade_outer(half, inner)
+    stack = jnp.zeros((OUTER, *got[0][1].shape), jnp.bfloat16)
+    for place, block in got:
+        stack = lax.dynamic_update_index_in_dim(stack, block, place, 0)
+    joined = jnp.concatenate([stack[z] for z in range(OUTER)], axis=axis)
+    return joined.astype(jnp.float32)
 
 
 def body(
@@ -149,7 +208,9 @@
     queries_low = rotate(to_heads(q_unit * gain_query), offsets, 1.0).astype(jnp.bfloat16)
     keys_low = rotate(to_heads(k_unit * gain_key), offsets, 1.0).astype(jnp.bfloat16)
     values_heads = to_heads(values_low)
-    mixed_heads, log_total = lax.map(attend, (queries_low, keys_low, values_heads, segment))
+    mixed_heads, log_total = jax.vmap(lambda *a: attend(a))(
+        queries_low, keys_low, values_heads, segment
+    )
     mixed_low = mixed_heads.reshape(row_count, local_width)
     attn_out = lax.psum_scatter(
         jnp.dot(mixed_low, w_out, preferred_element_type=jnp.float32).astype(jnp.bfloat16),
@@ -160,7 +221,17 @@
     a_inv = lax.rsqrt(jnp.mean(attn_out * attn_out, axis=1, keepdims=True) + EPS)
     a_unit = attn_out * a_inv
     hidden = tokens.astype(jnp.float32) + a_unit * gain_attn
-    hidden_all = lax.all_gather(hidden.astype(jnp.bfloat16), "tensor", axis=0, tiled=True)
+    hidden_low = hidden.astype(jnp.bfloat16)
+    hidden_all = lax.all_gather(hidden_low, "tensor", axis=0, tiled=True)
+    inner_count = lax.axis_size("dp") // OUTER
+    outer_index = lax.axis_index("dp") // inner_count
+
+    def gather_group(shard):
+        groups = [[z * inner_count + i for z in range(OUTER)] for i in range(inner_count)]
+        part = lax.all_gather(shard, "dp", axis=0, tiled=True, axis_index_groups=groups)
+        return lax.all_gather(part, "tensor", axis=0, tiled=True)
+
+    hidden_group = gather_group(hidden_low)
     gate_acts = jnp.dot(hidden_all, w_gate, preferred_element_type=jnp.float32)
     up_acts = jnp.dot(hidden_all, w_up, preferred_element_type=jnp.float32)
     gate_sigmoid = jax.nn.sigmoid(gate_acts)
@@ -176,15 +247,30 @@
     output = (hidden + f_unit * gain_mlp).astype(jnp.bfloat16)
     grad_output = cotangent.astype(jnp.float32)
     grad_mlp, grad_gain_mlp_part = post_norm_back(grad_output, f_unit, f_inv, gain_mlp)
-    mlp_grad_all = lax.all_gather(grad_mlp.astype(jnp.bfloat16), "tensor", axis=0, tiled=True)
-    grad_w_down = t_times(inner_low, mlp_grad_all)
+    grad_mlp_low = grad_mlp.astype(jnp.bfloat16)
+    mlp_grad_all = lax.all_gather(grad_mlp_low, "tensor", axis=0, tiled=True)
+    mlp_grad_group = gather_group(grad_mlp_low)
     grad_inner = times_t(mlp_grad_all, w_down)
     grad_gate_low = (
         grad_inner * up_acts * gate_sigmoid * (1.0 + gate_acts * (1.0 - gate_sigmoid))
     ).astype(jnp.bfloat16)
     grad_up_low = (grad_inner * gate_acts * gate_sigmoid).astype(jnp.bfloat16)
-    grad_w_gate = t_times(hidden_all, grad_gate_low)
-    grad_w_up = t_times(hidden_all, grad_up_low)
+    part_width = w_gate.shape[1] // OUTER
+    gate_part = lax.dynamic_slice_in_dim(w_gate, outer_index * part_width, part_width, 1)
+    up_part = lax.dynamic_slice_in_dim(w_up, outer_index * part_width, part_width, 1)
+    down_part = lax.dynamic_slice_in_dim(w_down, outer_index * part_width, part_width, 0)
+    gate_g = jnp.dot(hidden_group, gate_part, preferred_element_type=jnp.float32)
+    up_g = jnp.dot(hidden_group, up_part, preferred_element_type=jnp.float32)
+    sig_g = jax.nn.sigmoid(gate_g)
+    inner_g = (gate_g * sig_g * up_g).astype(jnp.bfloat16)
+    grad_inner_g = times_t(mlp_grad_group, down_part)
+    grad_gate_g = (grad_inner_g * up_g * sig_g * (1.0 + gate_g * (1.0 - sig_g))).astype(
+        jnp.bfloat16
+    )
+    grad_up_g = (grad_inner_g * gate_g * sig_g).astype(jnp.bfloat16)
+    sum_down = scatter_join(split_cols(t_times(inner_g, mlp_grad_group), inner_count), inner_count, 0)
+    sum_gate = scatter_join(split_rows(t_times(hidden_group, grad_gate_g), inner_count), inner_count, 1)
+    sum_up = scatter_join(split_rows(t_times(hidden_group, grad_up_g), inner_count), inner_count, 1)
     grad_hidden = grad_output + lax.psum_scatter(
         (times_t(grad_gate_low, w_gate) + times_t(grad_up_low, w_up)).astype(jnp.bfloat16),
         "tensor",
@@ -195,8 +281,8 @@
     attn_grad_all = lax.all_gather(grad_attn.astype(jnp.bfloat16), "tensor", axis=0, tiled=True)
     grad_w_out = t_times(mixed_low, attn_grad_all)
     grad_mixed = times_t(attn_grad_all, w_out).astype(jnp.bfloat16)
-    grad_q_rot, grad_k_rot, grad_values_low = lax.map(
-        attend_back, (queries_low, keys_low, values_heads, segment, log_total, to_heads(grad_mixed))
+    grad_q_rot, grad_k_rot, grad_values_low = jax.vmap(lambda *a: attend_back(a))(
+        queries_low, keys_low, values_heads, segment, log_total, to_heads(grad_mixed)
     )
     grad_q_norm = rotate(grad_q_rot, offsets, -1.0).reshape(row_count, local_width)
     grad_k_norm = rotate(grad_k_rot, offsets, -1.0).reshape(row_count, local_width)
@@ -239,27 +325,13 @@
     grad_gain_query = lax.dynamic_slice(gain_total[0], (tensor_start,), (local_width,))
     grad_gain_key = lax.dynamic_slice(gain_total[1], (tensor_start,), (local_width,))
     summed = (
-        lax.psum_scatter(
-            grad_w_query.astype(jnp.bfloat16), "dp", scatter_dimension=0, tiled=True
-        ).astype(jnp.float32),
-        lax.psum_scatter(
-            grad_w_key.astype(jnp.bfloat16), "dp", scatter_dimension=0, tiled=True
-        ).astype(jnp.float32),
-        lax.psum_scatter(
-            grad_w_value.astype(jnp.bfloat16), "dp", scatter_dimension=0, tiled=True
-        ).astype(jnp.float32),
-        lax.psum_scatter(
-            grad_w_out.astype(jnp.bfloat16), "dp", scatter_dimension=1, tiled=True
-        ).astype(jnp.float32),
-        lax.psum_scatter(
-            grad_w_gate.astype(jnp.bfloat16), "dp", scatter_dimension=0, tiled=True
-        ).astype(jnp.float32),
-        lax.psum_scatter(
-            grad_w_up.astype(jnp.bfloat16), "dp", scatter_dimension=0, tiled=True
-        ).astype(jnp.float32),
-        lax.psum_scatter(
-            grad_w_down.astype(jnp.bfloat16), "dp", scatter_dimension=1, tiled=True
-        ).astype(jnp.float32),
+        scatter_sum(split_rows(grad_w_query, inner_count), inner_count),
+        scatter_sum(split_rows(grad_w_key, inner_count), inner_count),
+        scatter_sum(split_rows(grad_w_value, inner_count), inner_count),
+        scatter_sum(split_cols(grad_w_out, inner_count), inner_count),
+        sum_gate,
+        sum_up,
+        sum_down,
     )
     return (
         output,

time: 1130 us -> 898 us (0.79)
  waiting for transfers between devices: 848 us -> 382 us
  local copies, waits for them, and re-layouts: 26.8 us -> 124 us
  starting transfers between devices: 1.87 us -> 72.1 us
  blocking collectives: 52.4 us -> 84.9 us
  matrix products: 125 us -> 149 us
    reduce_scatter x7 -> x0, waiting for transfers between devices: 630 us -> none  [the longest x1 151 us: body(): lax.psum_scatter(grad_w_gate.astype(jnp.bfloat16), 'dp', scatter_dimensio...]
    all_gather x2 -> x6, waiting for transfers between devices: 44.8 us -> 152 us  [the longest x2 58.4 us: gather_group(): return lax.all_gather(part, 'tensor', axis=0, tiled=True)]
    ppermute x0 -> x28, waiting for transfers between devices: none -> 86.7 us  [swap(): return lax.ppermute(value, 'dp', [(d, d ^ shift) for d in range(size)])]
    ppermute x0 -> x28, starting transfers between devices: none -> 71.1 us  [swap(): return lax.ppermute(value, 'dp', [(d, d ^ shift) for d in range(size)])]
    another operation x0 -> x12, local copies, waits for them, and re-layouts: none -> 42.2 us
    psum x1, blocking collectives: 40.7 us -> 72.5 us  [body(): gain_total = lax.psum(gain_stack, ('dp', 'tensor'))]
    reduce_scatter x1, waiting for transfers between devices: 31.8 us -> 0.01 us  [body(): lax.psum_scatter((times_t(grad_queries_low, w_query) + times_t(grad_keys_...]
    reshape x0 -> x4, local copies, waits for them, and re-layouts: none -> 27.1 us  [the longest x3 20.2 us: split_rows(): return grad.reshape(OUTER, inner, -1, cols).transpose(1, 0, 2, 3)]
  transfers between devices with their start and end apart: 15 -> 40, of which waited for: 14 -> 18; matrix products, arithmetic and copies ran while one was open for 6% -> 23% of each run, Pallas kernels for 0% -> 0%
where the time goes in v1:
time: 898 us; the launch traced here: 885 us
  waiting for transfers between devices  382 us (43%)
  matrix products  149 us (17%)
  local copies, waits for them, and re-layouts  124 us (14%)
  blocking collectives  84.9 us (9%)
  starting transfers between devices  72.1 us (8%)
  other arithmetic  56.6 us (6%)
  between operations  16 us (2%)
    ppermute x28, waiting for transfers between devices, swap(): return lax.ppermute(value, 'dp', [(d, d ^ shift) for d in range(size)])  86.7 us
    psum x1, blocking collectives, body(): gain_total = lax.psum(gain_stack, ('dp', 'tensor'))  72.5 us
    ppermute x28, starting transfers between devices, swap(): return lax.ppermute(value, 'dp', [(d, d ^ shift) for d in range(size)])  71.1 us
    all_gather x2, waiting for transfers between devices, gather_group(): return lax.all_gather(part, 'tensor', axis=0, tiled=True)  58.4 us
    dot_general x8, matrix products, times_t(): lax.dot_general(left_mat, right_mat, (((1,), (1,)), ((), ())), preferred_...  49.8 us
    all_gather x2, waiting for transfers between devices, gather_group(): lax.all_gather(shard, 'dp', axis=0, tiled=True, axis_index_groups=groups)  48.5 us
    another operation x12, local copies, waits for them, and re-layouts  42.2 us
    dot_general x7, matrix products, t_times(): lax.dot_general(left_mat, right_mat, (((0,), (0,)), ((), ())), preferred_...  36.4 us
  transfers between devices with their start and end apart: 40, of which 18 were waited for; matrix products, arithmetic and copies ran while one was open for 23% of the time, Pallas kernels for 0%

profile of v1, /device:TPU:0, one launch (start us, length us, event | category | flops | bytes accessed | tf_op | source)
XLA Modules:
  0.0 884.8 jit_solution(406805340475882868)
XLA Ops:
  12.2 22.7 %all-gather.9.cloned.1.call-done = bf16[512,2048]{1,0:T(8,128)(2,1)} async-done(((bf16[128,2048]{1,0:T(8,128)(2,1)}), bf16[512,2048]{1,0:T(8,128)(2,1)}) %all-gather.9.cloned.1.call-update) | async-done | bytes 2097168 | tf_op jit(solution)/shard_map/all_gather | solution.py:191
  34.9 4.0 multiply_reduce_fusion.4
  40.3 5.9 all-reduce.1
  59.2 2.5 fusion.64
  69.3 2.6 convolution_convert_fusion.1
  72.0 32.6 %reduce-scatter.5.cloned.1.call-done = bf16[128,2048]{1,0:T(8,128)(2,1)} async-done(((bf16[512,2048]{1,0:T(8,128)(2,1)}), bf16[128,2048]{1,0:T(8,128)(2,1)}) %reduce-scatter.5.cloned.1.call-update) | async-done | bytes 524304 | tf_op jit(solution)/shard_map/reduce_scatter | solution.py:215
  108.4 22.4 %all-gather.11.cloned.1.call-done = bf16[512,2048]{1,0:T(8,128)(2,1)} async-done(((bf16[128,2048]{1,0:T(8,128)(2,1)}), bf16[512,2048]{1,0:T(8,128)(2,1)}) %all-gather.11.cloned.1.call-update) | async-done | bytes 2097168 | tf_op jit(solution)/shard_map/all_gather | solution.py:225
  130.7 8.6 fusion.92
  139.3 8.4 fusion.93
  149.8 9.5 %convolution_convert_fusion = bf16[512,2048]{1,0:T(8,128)(2,1)} fusion(bf16[2048,2048]{1,0:T(8,128)(2,1)} %param.22, f32[512,2048]{1,0:T(8,128)S(1)} %fusion.93, f32[512,2048]{1,0:T(8,128)S(1)} %fusion.92), kind=kOutput, calls=%fused_computation.21 | convolution fusion | flops 4302307328 | bytes 18874368 | tf_op jit(solution)/shard_map/dot_general | solution.py:240
  159.3 31.5 %reduce-scatter.7.cloned.1.call-done = bf16[128,2048]{1,0:T(8,128)(2,1)} async-done(((bf16[512,2048]{1,0:T(8,128)(2,1)}), bf16[128,2048]{1,0:T(8,128)(2,1)}) %reduce-scatter.7.cloned.1.call-update) | async-done | bytes 524304 | tf_op jit(solution)/shard_map/reduce_scatter | solution.py:239
  195.9 22.7 %all-gather.13.cloned.1.call-done = bf16[512,2048]{1,0:T(8,128)(2,1)} async-done(((bf16[128,2048]{1,0:T(8,128)(2,1)}), bf16[512,2048]{1,0:T(8,128)(2,1)}) %all-gather.13.cloned.1.call-update) | async-done | bytes 2097168 | tf_op jit(solution)/shard_map/all_gather | solution.py:251
  218.6 7.6 fusion.94
  226.2 13.6 %fusion.25 = f32[512,2048]{1,0:T(8,128)} fusion(bf16[2048,2048]{1,0:T(8,128)(2,1)} %param.20, f32[512,2048]{1,0:T(8,128)} %copy-done.53, f32[512,2048]{1,0:T(8,128)S(1)} %fusion.94, f32[512,2048]{1,0:T(8,128)} %copy-done.54), kind=kOutput, calls=%fused_computation.56 | convolution fusion | flops 4305453056 | bytes 25165824 | tf_op jit(solution)/shard_map/dot_general | solution.py:53
  239.8 11.8 %add_convert_fusion.1 = bf16[512,2048]{1,0:T(8,128)(2,1)} fusion(f32[512,2048]{1,0:T(8,128)} %fusion.25, bf16[2048,2048]{1,0:T(8,128)(2,1)} %param.21, f32[512,2048]{1,0:T(8,128)S(1)} %fusion.94, f32[512,2048]{1,0:T(8,128)} %copy-done.53), kind=kOutput, calls=%fused_computation.8 | convolution fusion | flops 4303355904 | bytes 23068672 | tf_op jit(solution)/shard_map/dot_general | solution.py:53
  252.4 30.8 %reduce-scatter.9.cloned.1.call-done = bf16[128,2048]{1,0:T(8,128)(2,1)} async-done(((bf16[512,2048]{1,0:T(8,128)(2,1)}), bf16[128,2048]{1,0:T(8,128)(2,1)}) %reduce-scatter.9.cloned.1.call-update) | async-done | bytes 524304 | tf_op jit(solution)/shard_map/reduce_scatter | solution.py:274
  284.8 2.9 fusion.48
  288.5 42.9 %all-gather.17.cloned.1.call-done = bf16[512,2048]{1,0:T(8,128)(2,1)} async-done(((bf16[128,2048]{1,0:T(8,128)(2,1)}), bf16[512,2048]{1,0:T(8,128)(2,1)}) %all-gather.17.cloned.1.call-update) | async-done | bytes 2097168 | tf_op jit(solution)/shard_map/all_gather | solution.py:231
  331.7 23.3 %all-gather.15.cloned.1.call-done = bf16[512,2048]{1,0:T(8,128)(2,1)} async-done(((bf16[128,2048]{1,0:T(8,128)(2,1)}), bf16[512,2048]{1,0:T(8,128)(2,1)}) %all-gather.15.cloned.1.call-update) | async-done | bytes 2097168 | tf_op jit(solution)/shard_map/all_gather | solution.py:281
  355.0 3.7 convolution_convert_fusion.2
  370.0 2.9 pad_maximum_fusion.1
  372.8 2.5 copy.69
  379.1 6.5 all-reduce
  394.8 2.7 add_convert_fusion
  397.6 5.6 all-gather.21.cloned.1.call-done
  403.3 58.4 %all-gather.19.cloned.1.call-done = bf16[2048,2048]{1,0:T(8,128)(2,1)} async-done(((bf16[512,2048]{1,0:T(8,128)(2,1)}), bf16[2048,2048]{1,0:T(8,128)(2,1)}) %all-gather.19.cloned.1.call-update) | async-done | bytes 8388624 | tf_op jit(solution)/shard_map/all_gather | solution.py:232
  461.7 10.6 %fusion.14 = f32[2048,512]{1,0:T(8,128)} fusion(bf16[2048,2048]{1,0:T(8,128)(2,1)} %all-gather.19.cloned.1.call-done, bf16[2048,2048]{1,0:T(8,128)(2,1)} %param.20, s32[]{:T(128)S(6)} %select_n.141), kind=kOutput, calls=%fused_computation.44 | convolution fusion | flops 4294967296 | bytes 14680068 | tf_op jit(solution)/shard_map/dot_general | solution.py:262
  472.4 8.6 fusion.18
  481.0 3.2 convolution_bitcast_fusion.2
  484.2 6.6 reshape.572
  490.8 5.4 constant_dynamic-slice_fusion.8
  496.2 5.8 copy.99
  503.5 3.4 convolution_bitcast_fusion.1
  506.9 6.8 reshape.573
  513.7 5.5 constant_dynamic-slice_fusion.6
  519.2 5.8 copy.100
  525.6 3.2 convolution_bitcast_fusion
  528.8 6.7 reshape.574
  535.5 4.1 constant_dynamic-slice_fusion.4
  539.6 4.2 copy.101
  545.2 2.9 copy.94
  553.7 3.1 constant_dynamic-slice_fusion.7
  556.8 72.5 %psum.39 = f32[4,2048]{1,0:T(4,128)S(1)} all-reduce(f32[4,2048]{1,0:T(4,128)S(1)} %pad_maximum_fusion.8), channel_id=1, replica_groups=mesh['dp'=8,'tensor'=4] {'dp','tensor'}, use_global_device_ids=true, to_apply=%region_26.27 | all-reduce | flops 8192 | bytes 65536 | tf_op jit(solution)/shard_map/psum | solution.py:324
  630.0 5.4 constant_dynamic-slice_fusion.5
  636.0 4.4 copy.71
  640.4 6.0 copy.73
  646.4 4.6 copy.75
  665.1 11.7 %collective-permute-start.5 = (bf16[256,512]{1,0:T(8,128)(2,1)S(1)}, bf16[256,512]{1,0:T(8,128)(2,1)S(1)}, u32[]{:S(2)}, u32[]{:S(2)}) collective-permute-start(bf16[256,512]{1,0:T(8,128)(2,1)S(1)} %get-tuple-element.65), channel_id=1, source_target_pairs={{0,8},{4,12},{8,0},{12,4},{16,24},{20,28},{24,16},{28,20},{1,9},{5... | collective-permute-start | bytes 786440 | tf_op jit(solution)/shard_map/ppermute | solution.py:120
  676.8 14.4 %collective-permute-done.2 = bf16[256,512]{1,0:T(8,128)(2,1)S(1)} collective-permute-done((bf16[256,512]{1,0:T(8,128)(2,1)S(1)}, bf16[256,512]{1,0:T(8,128)(2,1)S(1)}, u32[]{:S(2)}, u32[]{:S(2)}) %collective-permute-start.2) | collective-permute-done | bytes 262176 | tf_op jit(solution)/shard_map/ppermute | solution.py:120
  692.9 15.7 %collective-permute-start.9 = (bf16[256,512]{1,0:T(8,128)(2,1)S(1)}, bf16[256,512]{1,0:T(8,128)(2,1)S(1)}, u32[]{:S(2)}, u32[]{:S(2)}) collective-permute-start(bf16[256,512]{1,0:T(8,128)(2,1)S(1)} %get-tuple-element.62), channel_id=1, source_target_pairs={{0,8},{4,12},{8,0},{12,4},{16,24},{20,28},{24,16},{28,20},{1,9},{5... | collective-permute-start | bytes 786440 | tf_op jit(solution)/shard_map/ppermute | solution.py:120
  709.5 4.2 collective-permute-done.6
  715.3 15.9 %collective-permute-start.13 = (bf16[512,256]{1,0:T(8,128)(2,1)S(1)}, bf16[512,256]{1,0:T(8,128)(2,1)S(1)}, u32[]{:S(2)}, u32[]{:S(2)}) collective-permute-start(bf16[512,256]{1,0:T(8,128)(2,1)S(1)} %get-tuple-element.59), channel_id=1, source_target_pairs={{0,8},{4,12},{8,0},{12,4},{16,24},{20,28},{24,16},{28,20},{1,9},{5... | collective-permute-start | bytes 786440 | tf_op jit(solution)/shard_map/ppermute | solution.py:120
  732.1 4.2 collective-permute-done.10
  737.2 8.4 collective-permute-done.14
  748.6 7.8 fusion.20
  756.4 7.7 fusion.26
  766.6 8.0 fusion.4
  778.9 9.7 %fusion.5 = f32[512,2048]{1,0:T(8,128)} fusion(bf16[2048,2048]{1,0:T(8,128)(2,1)S(1)} %bitcast.317, f32[2048,512]{1,0:T(8,128)} %fusion.18, f32[2048,512]{1,0:T(8,128)} %fusion.14), kind=kOutput, calls=%fused_computation.25 | convolution fusion | flops 4301258752 | bytes 20971520 | tf_op jit(solution)/shard_map/dot_general | solution.py:59
  788.6 6.9 reshape.577
  795.5 4.2 constant_dynamic-slice_fusion.1
  809.2 4.7 collective-permute-done.20
  814.6 19.0 %collective-permute-done.24 = bf16[4,512,256]{2,1,0:T(8,128)(2,1)S(1)} collective-permute-done((bf16[4,512,256]{2,1,0:T(8,128)(2,1)S(1)}, bf16[4,512,256]{2,1,0:T(8,128)(2,1)S(1)}, u32[]{:S(2)}, u32[]{:S(2)}) %collective-permute-start.24) | collective-permute-done | bytes 1048608 | tf_op jit(solution)/shard_map/ppermute | solution.py:120
  840.5 20.8 %collective-permute-done.22 = bf16[256,512]{1,0:T(8,128)(2,1)S(1)} collective-permute-done((bf16[256,512]{1,0:T(8,128)(2,1)S(1)}, bf16[256,512]{1,0:T(8,128)(2,1)S(1)}, u32[]{:S(2)}, u32[]{:S(2)}) %collective-permute-start.22) | collective-permute-done | bytes 262176 | tf_op jit(solution)/shard_map/ppermute | solution.py:120
  861.6 11.0 %collective-permute-done.26 = bf16[512,256]{1,0:T(8,128)(2,1)S(1)} collective-permute-done((bf16[512,256]{1,0:T(8,128)(2,1)S(1)}, bf16[512,256]{1,0:T(8,128)(2,1)S(1)}, u32[]{:S(2)}, u32[]{:S(2)}) %collective-permute-start.26) | collective-permute-done | bytes 262176 | tf_op jit(solution)/shard_map/ppermute | solution.py:120
  (294 shorter events, 127.2 us)
Async XLA Ops:
  7.2 27.7 %copy-start = (bf16[2048,512]{1,0:T(8,128)(2,1)S(1)}, bf16[2048,512]{1,0:T(8,128)(2,1)}, u32[]{:S(2)}) copy-start(bf16[2048,512]{1,0:T(8,128)(2,1)} %param.16) | copy-start | bytes 6291460
  7.2 27.7 %all-gather.9.cloned.1.call-start = ((), (), s32[]{:S(2)}) async-start(), calls=%async_computation.4 | async-start | bytes 2621440 | tf_op jit(solution)/shard_map/all_gather | solution.py:191
  7.9 96.7 %reduce-scatter.5.cloned.1.call-start = ((), (), s32[]{:S(2)}) async-start(), calls=%async_computation.5 | async-start | bytes 2621440 | tf_op jit(solution)/shard_map/reduce_scatter | solution.py:215
  40.2 13.2 %copy-start.14 = (f32[512,512]{0,1:T(8,128)}, f32[512,512]{0,1:T(8,128)S(1)}, u32[]{:S(2)}) copy-start(f32[512,512]{0,1:T(8,128)S(1)} %get-tuple-element.89) | copy-start | bytes 3145732
  40.3 13.0 %copy-start.49 = (f32[512]{0:T(512)S(1)}, f32[512]{0:T(512)}, u32[]{:S(2)}) copy-start(f32[512]{0:T(512)} %param.24) | copy-start | bytes 6148
  68.5 37.3 %copy-start.44 = (bf16[4,128,512]{2,1,0:T(8,128)(2,1)}, bf16[4,128,512]{2,1,0:T(8,128)(2,1)S(1)}, u32[]{:S(2)}) copy-start(bf16[4,128,512]{2,1,0:T(8,128)(2,1)S(1)} %fusion.40) | copy-start | bytes 1572868
  69.3 36.5 %copy-start.19 = (bf16[128,2048]{1,0:T(8,128)(2,1)S(1)}, bf16[128,2048]{1,0:T(8,128)(2,1)}, u32[]{:S(2)}) copy-start(bf16[128,2048]{1,0:T(8,128)(2,1)} %param.14) | copy-start | bytes 1572868
  69.3 36.5 %copy-start.46 = (f32[2048]{0:T(1024)S(1)}, f32[2048]{0:T(1024)}, u32[]{:S(2)}) copy-start(f32[2048]{0:T(1024)} %param.25) | copy-start | bytes 24580
  72.0 58.8 %all-gather.11.cloned.1.call-start = ((), (), s32[]{:S(2)}) async-start(), calls=%async_computation.6 | async-start | bytes 2621440 | tf_op jit(solution)/shard_map/all_gather | solution.py:225
  108.0 82.9 %reduce-scatter.7.cloned.1.call-start = ((), (), s32[]{:S(2)}) async-start(), calls=%async_computation.7 | async-start | bytes 2621440 | tf_op jit(solution)/shard_map/reduce_scatter | solution.py:239
  130.7 8.6 copy-start.52
  139.3 8.4 copy-start.53
  149.8 42.3 %copy-start.11 = (bf16[128,2048]{1,0:T(8,128)(2,1)S(1)}, bf16[128,2048]{1,0:T(8,128)(2,1)}, u32[]{:S(2)}) copy-start(bf16[128,2048]{1,0:T(8,128)(2,1)} %param.27) | copy-start | bytes 1572868
  149.8 42.3 %copy-start.47 = (f32[2048]{0:T(1024)S(1)}, f32[2048]{0:T(1024)}, u32[]{:S(2)}) copy-start(f32[2048]{0:T(1024)} %param.26) | copy-start | bytes 24580
  159.3 59.3 %all-gather.13.cloned.1.call-start = ((), (), s32[]{:S(2)}) async-start(), calls=%async_computation.8 | async-start | bytes 2621440 | tf_op jit(solution)/shard_map/all_gather | solution.py:251
  195.8 87.4 %reduce-scatter.9.cloned.1.call-start = ((), (), s32[]{:S(2)}) async-start(), calls=%async_computation.9 | async-start | bytes 2621440 | tf_op jit(solution)/shard_map/reduce_scatter | solution.py:274
  239.8 43.4 %copy-start.16 = (bf16[128,2048]{1,0:T(8,128)(2,1)S(1)}, bf16[128,2048]{1,0:T(8,128)(2,1)}, u32[]{:S(2)}) copy-start(bf16[128,2048]{1,0:T(8,128)(2,1)} %reduce-scatter.5.cloned.1.call-done) | copy-start | bytes 1572868
  251.6 79.8 %all-gather.17.cloned.1.call-start = ((), (), s32[]{:S(2)}) async-start(), calls=%async_computation.12 | async-start | bytes 2621440 | tf_op jit(solution)/shard_map/all_gather | solution.py:231
  252.4 102.6 %all-gather.15.cloned.1.call-start = ((), (), s32[]{:S(2)}) async-start(), calls=%async_computation.10 | async-start | bytes 2621440 | tf_op jit(solution)/shard_map/all_gather | solution.py:281
  287.7 115.5 %all-gather.21.cloned.1.call-start = ((), (), s32[]{:S(2)}) async-start(), calls=%async_computation.14 | async-start | bytes 2621440 | tf_op jit(solution)/shard_map/all_gather | solution.py:231
  288.5 173.2 %all-gather.19.cloned.1.call-start = ((), (), s32[]{:S(2)}) async-start(), calls=%async_computation.13 | async-start | bytes 10485760 | tf_op jit(solution)/shard_map/all_gather | solution.py:232
  331.4 415.0 %reduce-scatter.11.cloned.1.call-start = ((), (), s32[]{:S(2)}) async-start(), calls=%async_computation.11 | async-start | bytes 2621440 | tf_op jit(solution)/shard_map/reduce_scatter | solution.py:308
  397.5 351.0 %all-gather.23.cloned.1.call-start = ((), (), s32[]{:S(2)}) async-start(), calls=%async_computation.15 | async-start | bytes 10485760 | tf_op jit(solution)/shard_map/all_gather | solution.py:232
  461.7 10.6 %copy-start.50 = (bf16[2048,2048]{1,0:T(8,128)(2,1)S(1)}, bf16[2048,2048]{1,0:T(8,128)(2,1)}, u32[]{:S(2)}) copy-start(bf16[2048,2048]{1,0:T(8,128)(2,1)} %all-gather.19.cloned.1.call-done) | copy-start | bytes 25165828
  472.4 8.6 copy-start.7
  472.4 8.6 copy-start.18
  502.0 149.5 %collective-permute-start = (bf16[4,256,512]{2,1,0:T(8,128)(2,1)}, bf16[4,256,512]{2,1,0:T(8,128)(2,1)}, u32[]{:S(2)}, u32[]{:S(2)}) collective-permute-start(bf16[4,256,512]{2,1,0:T(8,128)(2,1)} %bitcast.298), channel_id=1, source_target_pairs={{0,4},{4,0},{8,12},{12,8},{16,20},{20,16},{24,28},{28,24},{1,5},{5... | collective-permute-start | bytes 3145736 | tf_op jit(solution)/shard_map/ppermute | solution.py:120
  513.7 11.9 %copy-start.21 = (bf16[4,128,512]{2,1,0:T(8,128)(2,1)S(1)}, bf16[4,128,512]{2,1,0:T(8,128)(2,1)}, u32[]{:S(2)}) copy-start(bf16[4,128,512]{2,1,0:T(8,128)(2,1)} %copy-done.20) | copy-start | bytes 1572868
  525.0 130.9 %collective-permute-start.4 = (bf16[4,256,512]{2,1,0:T(8,128)(2,1)}, bf16[4,256,512]{2,1,0:T(8,128)(2,1)}, u32[]{:S(2)}, u32[]{:S(2)}) collective-permute-start(bf16[4,256,512]{2,1,0:T(8,128)(2,1)} %bitcast.297), channel_id=1, source_target_pairs={{0,4},{4,0},{8,12},{12,8},{16,20},{20,16},{24,28},{28,24},{1,5},{5... | collective-permute-start | bytes 3145736 | tf_op jit(solution)/shard_map/ppermute | solution.py:120
  539.6 8.5 copy-start.45
  543.9 116.2 %collective-permute-start.8 = (bf16[4,256,512]{2,1,0:T(8,128)(2,1)}, bf16[4,256,512]{2,1,0:T(8,128)(2,1)}, u32[]{:S(2)}, u32[]{:S(2)}) collective-permute-start(bf16[4,256,512]{2,1,0:T(8,128)(2,1)} %bitcast.296), channel_id=1, source_target_pairs={{0,4},{4,0},{8,12},{12,8},{16,20},{20,16},{24,28},{28,24},{1,5},{5... | collective-permute-start | bytes 3145736 | tf_op jit(solution)/shard_map/ppermute | solution.py:120
  550.5 112.7 %collective-permute-start.12 = (bf16[4,512,256]{2,1,0:T(8,128)(2,1)}, bf16[4,512,256]{2,1,0:T(8,128)(2,1)}, u32[]{:S(2)}, u32[]{:S(2)}) collective-permute-start(bf16[4,512,256]{2,1,0:T(8,128)(2,1)} %fusion.56), channel_id=1, source_target_pairs={{0,4},{4,0},{8,12},{12,8},{16,20},{20,16},{24,28},{28,24},{1,5},{5... | collective-permute-start | bytes 3145736 | tf_op jit(solution)/shard_map/ppermute | solution.py:120
  653.9 11.2 %collective-permute-start.3 = (bf16[256,512]{1,0:T(8,128)(2,1)S(1)}, bf16[256,512]{1,0:T(8,128)(2,1)S(1)}, u32[]{:S(2)}, u32[]{:S(2)}) collective-permute-start(bf16[256,512]{1,0:T(8,128)(2,1)S(1)} %get-tuple-element.69), channel_id=1, source_target_pairs={{0,24},{4,28},{8,16},{12,20},{16,8},{20,12},{24,0},{28,4},{1,25},{... | collective-permute-start | bytes 786440 | tf_op jit(solution)/shard_map/ppermute | solution.py:120
  655.5 35.7 %collective-permute-start.2 = (bf16[256,512]{1,0:T(8,128)(2,1)S(1)}, bf16[256,512]{1,0:T(8,128)(2,1)S(1)}, u32[]{:S(2)}, u32[]{:S(2)}) collective-permute-start(bf16[256,512]{1,0:T(8,128)(2,1)S(1)} %get-tuple-element.70), channel_id=1, source_target_pairs={{0,16},{4,20},{8,24},{12,28},{16,0},{20,4},{24,8},{28,12},{1,17},{... | collective-permute-start | bytes 786440 | tf_op jit(solution)/shard_map/ppermute | solution.py:120
  655.9 36.9 %collective-permute-start.1 = (bf16[256,512]{1,0:T(8,128)(2,1)S(1)}, bf16[256,512]{1,0:T(8,128)(2,1)S(1)}, u32[]{:S(2)}, u32[]{:S(2)}) collective-permute-start(bf16[256,512]{1,0:T(8,128)(2,1)S(1)} %get-tuple-element.68), channel_id=1, source_target_pairs={{0,8},{4,12},{8,0},{12,4},{16,24},{20,28},{24,16},{28,20},{1,9},{5... | collective-permute-start | bytes 786440 | tf_op jit(solution)/shard_map/ppermute | solution.py:120
  660.0 32.9 %collective-permute-start.7 = (bf16[256,512]{1,0:T(8,128)(2,1)S(1)}, bf16[256,512]{1,0:T(8,128)(2,1)S(1)}, u32[]{:S(2)}, u32[]{:S(2)}) collective-permute-start(bf16[256,512]{1,0:T(8,128)(2,1)S(1)} %get-tuple-element.66), channel_id=1, source_target_pairs={{0,24},{4,28},{8,16},{12,20},{16,8},{20,12},{24,0},{28,4},{1,25},{... | collective-permute-start | bytes 786440 | tf_op jit(solution)/shard_map/ppermute | solution.py:120
  663.2 50.5 %collective-permute-start.6 = (bf16[256,512]{1,0:T(8,128)(2,1)S(1)}, bf16[256,512]{1,0:T(8,128)(2,1)S(1)}, u32[]{:S(2)}, u32[]{:S(2)}) collective-permute-start(bf16[256,512]{1,0:T(8,128)(2,1)S(1)} %get-tuple-element.67), channel_id=1, source_target_pairs={{0,16},{4,20},{8,24},{12,28},{16,0},{20,4},{24,8},{28,12},{1,17},{... | collective-permute-start | bytes 786440 | tf_op jit(solution)/shard_map/ppermute | solution.py:120
  665.0 81.4 %copy-start.22 = (bf16[128,2048]{1,0:T(8,128)(2,1)S(1)}, bf16[128,2048]{1,0:T(8,128)(2,1)}, u32[]{:S(2)}) copy-start(bf16[128,2048]{1,0:T(8,128)(2,1)} %reduce-scatter.9.cloned.1.call-done) | copy-start | bytes 1572868
  665.1 50.2 %collective-permute-start.5 = (bf16[256,512]{1,0:T(8,128)(2,1)S(1)}, bf16[256,512]{1,0:T(8,128)(2,1)S(1)}, u32[]{:S(2)}, u32[]{:S(2)}) collective-permute-start(bf16[256,512]{1,0:T(8,128)(2,1)S(1)} %get-tuple-element.65), channel_id=1, source_target_pairs={{0,8},{4,12},{8,0},{12,4},{16,24},{20,28},{24,16},{28,20},{1,9},{5... | collective-permute-start | bytes 786440 | tf_op jit(solution)/shard_map/ppermute | solution.py:120
  691.2 24.1 %collective-permute-start.11 = (bf16[256,512]{1,0:T(8,128)(2,1)S(1)}, bf16[256,512]{1,0:T(8,128)(2,1)S(1)}, u32[]{:S(2)}, u32[]{:S(2)}) collective-permute-start(bf16[256,512]{1,0:T(8,128)(2,1)S(1)} %get-tuple-element.63), channel_id=1, source_target_pairs={{0,24},{4,28},{8,16},{12,20},{16,8},{20,12},{24,0},{28,4},{1,25},{... | collective-permute-start | bytes 786440 | tf_op jit(solution)/shard_map/ppermute | solution.py:120
  692.8 43.4 %collective-permute-start.10 = (bf16[256,512]{1,0:T(8,128)(2,1)S(1)}, bf16[256,512]{1,0:T(8,128)(2,1)S(1)}, u32[]{:S(2)}, u32[]{:S(2)}) collective-permute-start(bf16[256,512]{1,0:T(8,128)(2,1)S(1)} %get-tuple-element.64), channel_id=1, source_target_pairs={{0,16},{4,20},{8,24},{12,28},{16,0},{20,4},{24,8},{28,12},{1,17},{... | collective-permute-start | bytes 786440 | tf_op jit(solution)/shard_map/ppermute | solution.py:120
  692.9 43.3 %collective-permute-start.9 = (bf16[256,512]{1,0:T(8,128)(2,1)S(1)}, bf16[256,512]{1,0:T(8,128)(2,1)S(1)}, u32[]{:S(2)}, u32[]{:S(2)}) collective-permute-start(bf16[256,512]{1,0:T(8,128)(2,1)S(1)} %get-tuple-element.62), channel_id=1, source_target_pairs={{0,8},{4,12},{8,0},{12,4},{16,24},{20,28},{24,16},{28,20},{1,9},{5... | collective-permute-start | bytes 786440 | tf_op jit(solution)/shard_map/ppermute | solution.py:120
  713.7 23.4 %collective-permute-start.15 = (bf16[512,256]{1,0:T(8,128)(2,1)S(1)}, bf16[512,256]{1,0:T(8,128)(2,1)S(1)}, u32[]{:S(2)}, u32[]{:S(2)}) collective-permute-start(bf16[512,256]{1,0:T(8,128)(2,1)S(1)} %get-tuple-element.60), channel_id=1, source_target_pairs={{0,24},{4,28},{8,16},{12,20},{16,8},{20,12},{24,0},{28,4},{1,25},{... | collective-permute-start | bytes 786440 | tf_op jit(solution)/shard_map/ppermute | solution.py:120
  715.3 30.3 %collective-permute-start.14 = (bf16[512,256]{1,0:T(8,128)(2,1)S(1)}, bf16[512,256]{1,0:T(8,128)(2,1)S(1)}, u32[]{:S(2)}, u32[]{:S(2)}) collective-permute-start(bf16[512,256]{1,0:T(8,128)(2,1)S(1)} %get-tuple-element.61), channel_id=1, source_target_pairs={{0,16},{4,20},{8,24},{12,28},{16,0},{20,4},{24,8},{28,12},{1,17},{... | collective-permute-start | bytes 786440 | tf_op jit(solution)/shard_map/ppermute | solution.py:120
  715.3 30.3 %collective-permute-start.13 = (bf16[512,256]{1,0:T(8,128)(2,1)S(1)}, bf16[512,256]{1,0:T(8,128)(2,1)S(1)}, u32[]{:S(2)}, u32[]{:S(2)}) collective-permute-start(bf16[512,256]{1,0:T(8,128)(2,1)S(1)} %get-tuple-element.59), channel_id=1, source_target_pairs={{0,8},{4,12},{8,0},{12,4},{16,24},{20,28},{24,16},{28,20},{1,9},{5... | collective-permute-start | bytes 786440 | tf_op jit(solution)/shard_map/ppermute | solution.py:120
  748.5 7.8 copy-start.56
  748.5 18.1 %slice-start = ((s8[8388608]{0:T(1024)(128)(4,1)}), s8[4194304]{0:T(1024)(128)(4,1)S(1)}, s32[]{:S(2)}) async-start(s8[8388608]{0:T(1024)(128)(4,1)} %bitcast.314), calls=%async_computation.16 | async-start | bytes 8388608
  756.3 10.3 %slice-start.1 = ((s8[8388608]{0:T(1024)(128)(4,1)}), s8[4194304]{0:T(1024)(128)(4,1)S(1)}, s32[]{:S(2)}) async-start(s8[8388608]{0:T(1024)(128)(4,1)} %bitcast.314), calls=%async_computation.17 | async-start | bytes 8388608
  764.0 10.6 %copy-start.34 = (f32[2048,512]{1,0:T(8,128)}, f32[2048,512]{1,0:T(8,128)S(1)}, u32[]{:S(2)}) copy-start(f32[2048,512]{1,0:T(8,128)S(1)} %fusion.26) | copy-start | bytes 12582916
  764.0 14.9 %slice-start.2 = ((s8[8388608]{0:T(1024)(128)(4,1)}), s8[4194304]{0:T(1024)(128)(4,1)S(1)}, s32[]{:S(2)}) async-start(s8[8388608]{0:T(1024)(128)(4,1)} %bitcast.316), calls=%async_computation.18 | async-start | bytes 8388608
  765.2 13.8 %slice-start.3 = ((s8[8388608]{0:T(1024)(128)(4,1)}), s8[4194304]{0:T(1024)(128)(4,1)S(1)}, s32[]{:S(2)}) async-start(s8[8388608]{0:T(1024)(128)(4,1)} %bitcast.316), calls=%async_computation.19 | async-start | bytes 8388608
  765.2 37.7 %collective-permute-start.16 = (bf16[4,256,512]{2,1,0:T(8,128)(2,1)}, bf16[4,256,512]{2,1,0:T(8,128)(2,1)}, u32[]{:S(2)}, u32[]{:S(2)}) collective-permute-start(bf16[4,256,512]{2,1,0:T(8,128)(2,1)} %fusion.58), channel_id=1, source_target_pairs={{0,4},{4,0},{8,12},{12,8},{16,20},{20,16},{24,28},{28,24},{1,5},{5... | collective-permute-start | bytes 3145736 | tf_op jit(solution)/shard_map/ppermute | solution.py:120
  777.7 36.2 %collective-permute-start.20 = (bf16[4,256,512]{2,1,0:T(8,128)(2,1)}, bf16[4,256,512]{2,1,0:T(8,128)(2,1)S(1)}, u32[]{:S(2)}, u32[]{:S(2)}) collective-permute-start(bf16[4,256,512]{2,1,0:T(8,128)(2,1)} %fusion.59), channel_id=1, source_target_pairs={{0,4},{4,0},{8,12},{12,8},{16,20},{20,16},{24,28},{28,24},{1,5},{5... | collective-permute-start | bytes 3145736 | tf_op jit(solution)/shard_map/ppermute | solution.py:120
  800.1 33.4 %collective-permute-start.24 = (bf16[4,512,256]{2,1,0:T(8,128)(2,1)S(1)}, bf16[4,512,256]{2,1,0:T(8,128)(2,1)S(1)}, u32[]{:S(2)}, u32[]{:S(2)}) collective-permute-start(bf16[4,512,256]{2,1,0:T(8,128)(2,1)S(1)} %bitcast.299), channel_id=1, source_target_pairs={{0,4},{4,0},{8,12},{12,8},{16,20},{20,16},{24,28},{28,24},{1,5},{5... | collective-permute-start | bytes 3145736 | tf_op jit(solution)/shard_map/ppermute | solution.py:120
  802.8 11.1 %copy-start.33 = (f32[2048,512]{1,0:T(8,128)S(1)}, f32[2048,512]{1,0:T(8,128)}, u32[]{:S(2)}) copy-start(f32[2048,512]{1,0:T(8,128)} %copy-done.32) | copy-start | bytes 12582916
  804.8 29.4 %collective-permute-start.17 = (bf16[256,512]{1,0:T(8,128)(2,1)S(1)}, bf16[256,512]{1,0:T(8,128)(2,1)S(1)}, u32[]{:S(2)}, u32[]{:S(2)}) collective-permute-start(bf16[256,512]{1,0:T(8,128)(2,1)S(1)} %get-tuple-element.57), channel_id=1, source_target_pairs={{0,8},{4,12},{8,0},{12,4},{16,24},{20,28},{24,16},{28,20},{1,9},{5... | collective-permute-start | bytes 786440 | tf_op jit(solution)/shard_map/ppermute | solution.py:120
  804.9 31.0 %collective-permute-start.18 = (bf16[256,512]{1,0:T(8,128)(2,1)S(1)}, bf16[256,512]{1,0:T(8,128)(2,1)S(1)}, u32[]{:S(2)}, u32[]{:S(2)}) collective-permute-start(bf16[256,512]{1,0:T(8,128)(2,1)S(1)} %get-tuple-element.56), channel_id=1, source_target_pairs={{0,16},{4,20},{8,24},{12,28},{16,0},{20,4},{24,8},{28,12},{1,17},{... | collective-permute-start | bytes 786440 | tf_op jit(solution)/shard_map/ppermute | solution.py:120
  807.0 30.9 %collective-permute-start.19 = (bf16[256,512]{1,0:T(8,128)(2,1)S(1)}, bf16[256,512]{1,0:T(8,128)(2,1)S(1)}, u32[]{:S(2)}, u32[]{:S(2)}) collective-permute-start(bf16[256,512]{1,0:T(8,128)(2,1)S(1)} %get-tuple-element.55), channel_id=1, source_target_pairs={{0,24},{4,28},{8,16},{12,20},{16,8},{20,12},{24,0},{28,4},{1,25},{... | collective-permute-start | bytes 786440 | tf_op jit(solution)/shard_map/ppermute | solution.py:120
  814.5 24.4 %collective-permute-start.21 = (bf16[256,512]{1,0:T(8,128)(2,1)S(1)}, bf16[256,512]{1,0:T(8,128)(2,1)S(1)}, u32[]{:S(2)}, u32[]{:S(2)}) collective-permute-start(bf16[256,512]{1,0:T(8,128)(2,1)S(1)} %get-tuple-element.49), channel_id=1, source_target_pairs={{0,8},{4,12},{8,0},{12,4},{16,24},{20,28},{24,16},{28,20},{1,9},{5... | collective-permute-start | bytes 786440 | tf_op jit(solution)/shard_map/ppermute | solution.py:120
  833.5 27.8 %collective-permute-start.22 = (bf16[256,512]{1,0:T(8,128)(2,1)S(1)}, bf16[256,512]{1,0:T(8,128)(2,1)S(1)}, u32[]{:S(2)}, u32[]{:S(2)}) collective-permute-start(bf16[256,512]{1,0:T(8,128)(2,1)S(1)} %get-tuple-element.48), channel_id=1, source_target_pairs={{0,16},{4,20},{8,24},{12,28},{16,0},{20,4},{24,8},{28,12},{1,17},{... | collective-permute-start | bytes 786440 | tf_op jit(solution)/shard_map/ppermute | solution.py:120
  834.2 27.2 %collective-permute-start.23 = (bf16[256,512]{1,0:T(8,128)(2,1)S(1)}, bf16[256,512]{1,0:T(8,128)(2,1)S(1)}, u32[]{:S(2)}, u32[]{:S(2)}) collective-permute-start(bf16[256,512]{1,0:T(8,128)(2,1)S(1)} %get-tuple-element.47), channel_id=1, source_target_pairs={{0,24},{4,28},{8,16},{12,20},{16,8},{20,12},{24,0},{28,4},{1,25},{... | collective-permute-start | bytes 786440 | tf_op jit(solution)/shard_map/ppermute | solution.py:120
  835.9 25.6 %collective-permute-start.25 = (bf16[512,256]{1,0:T(8,128)(2,1)S(1)}, bf16[512,256]{1,0:T(8,128)(2,1)S(1)}, u32[]{:S(2)}, u32[]{:S(2)}) collective-permute-start(bf16[512,256]{1,0:T(8,128)(2,1)S(1)} %get-tuple-element.41), channel_id=1, source_target_pairs={{0,8},{4,12},{8,0},{12,4},{16,24},{20,28},{24,16},{28,20},{1,9},{5... | collective-permute-start | bytes 786440 | tf_op jit(solution)/shard_map/ppermute | solution.py:120
  837.9 34.7 %collective-permute-start.26 = (bf16[512,256]{1,0:T(8,128)(2,1)S(1)}, bf16[512,256]{1,0:T(8,128)(2,1)S(1)}, u32[]{:S(2)}, u32[]{:S(2)}) collective-permute-start(bf16[512,256]{1,0:T(8,128)(2,1)S(1)} %get-tuple-element.40), channel_id=1, source_target_pairs={{0,16},{4,20},{8,24},{12,28},{16,0},{20,4},{24,8},{28,12},{1,17},{... | collective-permute-start | bytes 786440 | tf_op jit(solution)/shard_map/ppermute | solution.py:120
  838.9 33.8 %collective-permute-start.27 = (bf16[512,256]{1,0:T(8,128)(2,1)S(1)}, bf16[512,256]{1,0:T(8,128)(2,1)S(1)}, u32[]{:S(2)}, u32[]{:S(2)}) collective-permute-start(bf16[512,256]{1,0:T(8,128)(2,1)S(1)} %get-tuple-element.39), channel_id=1, source_target_pairs={{0,24},{4,28},{8,16},{12,20},{16,8},{20,12},{24,0},{28,4},{1,25},{... | collective-permute-start | bytes 786440 | tf_op jit(solution)/shard_map/ppermute | solution.py:120
  (37 other events, 128.5 us)
Sparse Core Ops, SparseCore 0:
  9.6 25.2 all-gather.8
  72.1 32.4 reduce-scatter.4
  108.1 22.5 all-gather.10
  159.4 31.4 reduce-scatter.6
  195.9 22.5 all-gather.12
  251.8 31.4 reduce-scatter.8
  285.5 45.9 all-gather.16
  333.6 21.3 all-gather.14
  357.2 45.9 all-gather.20
  404.7 56.9 all-gather.18
  465.0 31.4 reduce-scatter.10
  497.9 58.2 all-gather.22

commit v2 on v1

--- a/solution.py
+++ b/solution.py
@@ -3,6 +3,8 @@
 import jax
 import jax.numpy as jnp
 from jax import lax
+from jax.experimental import pallas as pl
+from jax.experimental.pallas import tpu as pltpu
 from jax.sharding import PartitionSpec as P
 
 HD = 128
@@ -166,6 +168,268 @@
         stack = lax.dynamic_update_index_in_dim(stack, block, place, 0)
     joined = jnp.concatenate([stack[z] for z in range(OUTER)], axis=axis)
     return joined.astype(jnp.float32)
+
+
+MESH = pl.DeviceIdType.MESH
+FULL = pl.BlockSpec(memory_space=pl.ANY)
+
+
+def grads_kernel(
+    hid_ref, dml_ref, hall_ref, dall_ref, wg_ref, wu_ref, wd_ref, tok_ref, dat_ref, dq_ref, dk_ref, dv_ref, mix_ref,
+    out_ref, gh_ref, gm_ref,
+    rows_v, wg_v, wu_v, wd_v, lhs_in, lhs_t, acc, full, part,
+    ld_sem, zs_s, zs_r, xs_s, xs_r, cs_s, cs_r, ys_s, ys_r, ts_s, ts_r, own_s,
+):
+    d = lax.axis_index("dp")
+    t = lax.axis_index("tensor")
+    z = d // 2
+    y = d % 2
+    mate = t + 1 - 2 * (t % 2)
+    across = (t + 2) % 4
+    far = (mate + 2) % 4
+    twin = z * 2 + 1 - y
+
+    def remote(src, dst, ss, rs, dd, tt):
+        return pltpu.make_async_remote_copy(
+            src_ref=src, dst_ref=dst, send_sem=ss, recv_sem=rs, device_id=(dd, tt), device_id_type=MESH
+        )
+
+    def peer(k):
+        return ((z + k) % 4) * 2 + y
+
+    f = wg_v.shape[1]
+    loads = [
+        pltpu.make_async_copy(tok_ref, rows_v.at[1, 0], ld_sem.at[0]),
+        pltpu.make_async_copy(dat_ref, rows_v.at[1, 1], ld_sem.at[1]),
+        pltpu.make_async_copy(dv_ref, lhs_in.at[0], ld_sem.at[2]),
+        pltpu.make_async_copy(dq_ref, lhs_in.at[1], ld_sem.at[3]),
+        pltpu.make_async_copy(dk_ref, lhs_in.at[2], ld_sem.at[4]),
+        pltpu.make_async_copy(mix_ref, lhs_in.at[3], ld_sem.at[5]),
+        pltpu.make_async_copy(hall_ref, rows_v.at[0, 0], ld_sem.at[6]),
+        pltpu.make_async_copy(dall_ref, rows_v.at[0, 1], ld_sem.at[7]),
+        pltpu.make_async_copy(wg_ref.at[:, pl.ds(z * f, f)], wg_v, ld_sem.at[8]),
+        pltpu.make_async_copy(wu_ref.at[:, pl.ds(z * f, f)], wu_v, ld_sem.at[9]),
+        pltpu.make_async_copy(wd_ref.at[pl.ds(z * f, f), :], wd_v, ld_sem.at[10]),
+    ]
+    for c in loads:
+        c.start()
+
+    barrier = pltpu.get_barrier_semaphore()
+    for dd, tt in [(peer(1), t), (peer(2), t), (peer(3), t), (twin, t), (d, mate), (d, across)]:
+        pl.semaphore_signal(barrier, inc=1, device_id=(dd, tt), device_id_type=MESH)
+    pl.semaphore_wait(barrier, 6)
+
+    shards = (hid_ref, dml_ref)
+    groups = (gh_ref, gm_ref)
+
+    def gather_z(a, k):
+        return remote(shards[a], groups[a].at[z, t], zs_s.at[a, k - 1], zs_r.at[a, k - 1], peer(k), t)
+
+    def forward_x(a, k):
+        r = (z + 4 - k) % 4
+        return remote(groups[a].at[r, t], groups[a].at[r, t], xs_s.at[a, k - 1], xs_r.at[a, k - 1], d, across)
+
+    def forward_c(a, k, h):
+        r = (z + 4 - k) % 4
+        q = t if h == 0 else across
+        return remote(groups[a].at[r, q], groups[a].at[r, q], cs_s.at[a, k - 1, h], cs_r.at[a, k - 1, h], d, mate)
+
+    order = (1, 3, 2)
+    for k in order:
+        for a in range(2):
+            gather_z(a, k).start()
+
+    def swap_y(w):
+        return remote(full.at[w, :, 1 - y], part.at[w], ys_s.at[w], ys_r.at[w], twin, t)
+
+    def trade_z(w, k):
+        return remote(
+            part.at[w, (z + k) % 4], out_ref.at[w, z], ts_s.at[w, k - 1], ts_r.at[w, k - 1], peer(k), t
+        )
+
+    def keep(w):
+        return pltpu.make_async_copy(part.at[w, z], out_ref.at[w, z], own_s.at[w])
+
+    def finish_y(w):
+        swap_y(w).wait()
+        for b in range(4):
+            part[w, b] = (part[w, b].astype(jnp.float32) + full[w, b, y].astype(jnp.float32)).astype(
+                jnp.bfloat16
+            )
+        for k in (2, 1, 3):
+            trade_z(w, k).start()
+        keep(w).start()
+
+    width = full.shape[4]
+
+    def attn_grad(w, side):
+        lhs_t[0] = lhs_in[w].astype(jnp.float32).T.astype(jnp.bfloat16)
+
+        def tile(j, carry):
+            cols = pl.ds(pl.multiple_of(j * width, width), width)
+            full[w, j // 2, j % 2] = jnp.dot(
+                lhs_t[0], rows_v[1, side, :, cols], preferred_element_type=jnp.float32
+            ).astype(jnp.bfloat16)
+            return carry
+
+        lax.fori_loop(0, 8, tile, 0)
+        swap_y(w).start()
+
+    loads[1].wait()
+    loads[5].wait()
+    attn_grad(3, 1)
+    for i in (0, 2, 3, 4):
+        loads[i].wait()
+    for w in range(3):
+        attn_grad(w, 0)
+
+    step = 256
+
+    def mlp_row(slot, first):
+        def wide(j, carry):
+            cols = pl.ds(pl.multiple_of(j * step, step), step)
+            g = jnp.dot(rows_v[slot, 0], wg_v[:, cols], preferred_element_type=jnp.float32)
+            u = jnp.dot(rows_v[slot, 0], wu_v[:, cols], preferred_element_type=jnp.float32)
+            di = lax.dot_general(
+                rows_v[slot, 1], wd_v[cols, :], (((1,), (1,)), ((), ())), preferred_element_type=jnp.float32
+            )
+            sg = jax.nn.sigmoid(g)
+            gs = g * sg
+            lhs_t[0, cols, :] = (gs * u).T.astype(jnp.bfloat16)
+            lhs_t[1, cols, :] = (di * u * sg * (1.0 + g * (1.0 - sg))).T.astype(jnp.bfloat16)
+            lhs_t[2, cols, :] = (di * gs).T.astype(jnp.bfloat16)
+            return carry
+
+        lax.fori_loop(0, f // step, wide, 0)
+
+        def deep(j, carry):
+            cols = pl.ds(pl.multiple_of(j * step, step), step)
+            for w, side in ((0, 1), (1, 0), (2, 0)):
+                new = jnp.dot(lhs_t[w], rows_v[slot, side, :, cols], preferred_element_type=jnp.float32)
+                if first:
+                    acc[w, :, cols] = new
+                else:
+                    acc[w, :, cols] += new
+            return carry
+
+        lax.fori_loop(0, acc.shape[2] // step, deep, 0)
+
+    for i in range(6, 11):
+        loads[i].wait()
+    mlp_row(0, True)
+
+    def advance_x(k):
+        for a in range(2):
+            gather_z(a, k).wait_recv()
+            forward_x(a, k).start()
+
+    def advance_c(k):
+        for a in range(2):
+            forward_x(a, k).wait_recv()
+            for h in range(2):
+                forward_c(a, k, h).start()
+
+    def row_loads(k, slot):
+        r = (z + 4 - k) % 4
+        return [
+            pltpu.make_async_copy(groups[a].at[r, q], rows_v.at[slot, a, pl.ds(q * 128, 128)], ld_sem.at[a * 4 + q])
+            for a in range(2)
+            for q in range(4)
+        ]
+
+    advance_x(order[0])
+    finish_y(3)
+    advance_c(order[0])
+    advance_x(order[1])
+    finish_y(0)
+    for n, k in enumerate(order):
+        slot = (n + 1) % 2
+        for a in range(2):
+            for h in range(2):
+                forward_c(a, k, h).wait_recv()
+        copies = row_loads(k, slot)
+        for c in copies:
+            c.start()
+        if n + 1 < 3:
+            advance_c(order[n + 1])
+        if n + 2 < 3:
+            advance_x(order[n + 2])
+        for c in copies:
+            c.wait()
+        mlp_row(slot, False)
+        if n < 2:
+            finish_y(n + 1)
+
+    def emit(w):
+        def tile(j, carry):
+            cols = pl.ds(pl.multiple_of(j * width, width), width)
+            full[4 + w, j // 2, j % 2] = acc[w, :, cols].astype(jnp.bfloat16)
+            return carry
+
+        lax.fori_loop(0, 8, tile, 0)
+        swap_y(4 + w).start()
+
+    for w in range(3):
+        emit(w)
+    for w in range(3):
+        finish_y(4 + w)
+    for k in order:
+        for a in range(2):
+            gather_z(a, k).wait_send()
+            forward_x(a, k).wait_send()
+            for h in range(2):
+                forward_c(a, k, h).wait_send()
+    for w in range(7):
+        keep(w).wait()
+        for k in range(1, 4):
+            trade_z(w, k).wait()
+
+
+def weight_grads(hid, dml, hall, dall, wg, wu, wd, tok, dat, dq, dk, dv, mix):
+    rows, width = hall.shape
+    f = wg.shape[1] // 4
+    block = width // 8
+    bf = jnp.bfloat16
+    dma = pltpu.SemaphoreType.DMA
+    flops = 2 * rows * width * f * (4 + 24)
+    return pl.pallas_call(
+        grads_kernel,
+        name="weight_grads",
+        out_shape=(
+            jax.ShapeDtypeStruct((7, 4, f, block), bf),
+            jax.ShapeDtypeStruct((4, 4, rows // 4, width), bf),
+            jax.ShapeDtypeStruct((4, 4, rows // 4, width), bf),
+        ),
+        in_specs=[FULL] * 13,
+        out_specs=(FULL,) * 3,
+        scratch_shapes=[
+            pltpu.VMEM((2, 2, rows, width), bf),
+            pltpu.VMEM((width, f), bf),
+            pltpu.VMEM((width, f), bf),
+            pltpu.VMEM((f, width), bf),
+            pltpu.VMEM((4, rows, f), bf),
+            pltpu.VMEM((3, f, rows), bf),
+            pltpu.VMEM((3, f, width), jnp.float32),
+            pltpu.VMEM((7, 4, 2, f, block), bf),
+            pltpu.VMEM((7, 4, f, block), bf),
+            dma((11,)),
+            dma((2, 3)),
+            dma((2, 3)),
+            dma((2, 3)),
+            dma((2, 3)),
+            dma((2, 3, 2)),
+            dma((2, 3, 2)),
+            dma((7,)),
+            dma((7,)),
+            dma((7, 3)),
+            dma((7, 3)),
+            dma((7,)),
+        ],
+        compiler_params=pltpu.CompilerParams(
+            collective_id=0, has_side_effects=True, vmem_limit_bytes=60 * 1024 * 1024
+        ),
+        cost_estimate=pl.CostEstimate(flops=flops, bytes_accessed=60 * 1024 * 1024, transcendentals=0),
+    )(hid, dml, hall, dall, wg, wu, wd, tok, dat, dq, dk, dv, mix)
 
 
 def body(
@@ -231,7 +495,9 @@
         part = lax.all_gather(shard, "dp", axis=0, tiled=True, axis_index_groups=groups)
         return lax.all_gather(part, "tensor", axis=0, tiled=True)
 
-    hidden_group = gather_group(hidden_low)
+    fused = lax.axis_size("dp") == 8
+    if not fused:
+        hidden_group = gather_group(hidden_low)
     gate_acts = jnp.dot(hidden_all, w_gate, preferred_element_type=jnp.float32)
     up_acts = jnp.dot(hidden_all, w_up, preferred_element_type=jnp.float32)
     gate_sigmoid = jax.nn.sigmoid(gate_acts)
@@ -249,28 +515,30 @@
     grad_mlp, grad_gain_mlp_part = post_norm_back(grad_output, f_unit, f_inv, gain_mlp)
     grad_mlp_low = grad_mlp.astype(jnp.bfloat16)
     mlp_grad_all = lax.all_gather(grad_mlp_low, "tensor", axis=0, tiled=True)
-    mlp_grad_group = gather_group(grad_mlp_low)
+    if not fused:
+        mlp_grad_group = gather_group(grad_mlp_low)
     grad_inner = times_t(mlp_grad_all, w_down)
     grad_gate_low = (
         grad_inner * up_acts * gate_sigmoid * (1.0 + gate_acts * (1.0 - gate_sigmoid))
     ).astype(jnp.bfloat16)
     grad_up_low = (grad_inner * gate_acts * gate_sigmoid).astype(jnp.bfloat16)
-    part_width = w_gate.shape[1] // OUTER
-    gate_part = lax.dynamic_slice_in_dim(w_gate, outer_index * part_width, part_width, 1)
-    up_part = lax.dynamic_slice_in_dim(w_up, outer_index * part_width, part_width, 1)
-    down_part = lax.dynamic_slice_in_dim(w_down, outer_index * part_width, part_width, 0)
-    gate_g = jnp.dot(hidden_group, gate_part, preferred_element_type=jnp.float32)
-    up_g = jnp.dot(hidden_group, up_part, preferred_element_type=jnp.float32)
-    sig_g = jax.nn.sigmoid(gate_g)
-    inner_g = (gate_g * sig_g * up_g).astype(jnp.bfloat16)
-    grad_inner_g = times_t(mlp_grad_group, down_part)
-    grad_gate_g = (grad_inner_g * up_g * sig_g * (1.0 + gate_g * (1.0 - sig_g))).astype(
-        jnp.bfloat16
-    )
-    grad_up_g = (grad_inner_g * gate_g * sig_g).astype(jnp.bfloat16)
-    sum_down = scatter_join(split_cols(t_times(inner_g, mlp_grad_group), inner_count), inner_count, 0)
-    sum_gate = scatter_join(split_rows(t_times(hidden_group, grad_gate_g), inner_count), inner_count, 1)
-    sum_up = scatter_join(split_rows(t_times(hidden_group, grad_up_g), inner_count), inner_count, 1)
+    if not fused:
+        part_width = w_gate.shape[1] // OUTER
+        gate_part = lax.dynamic_slice_in_dim(w_gate, outer_index * part_width, part_width, 1)
+        up_part = lax.dynamic_slice_in_dim(w_up, outer_index * part_width, part_width, 1)
+        down_part = lax.dynamic_slice_in_dim(w_down, outer_index * part_width, part_width, 0)
+        gate_g = jnp.dot(hidden_group, gate_part, preferred_element_type=jnp.float32)
+        up_g = jnp.dot(hidden_group, up_part, preferred_element_type=jnp.float32)
+        sig_g = jax.nn.sigmoid(gate_g)
+        inner_g = (gate_g * sig_g * up_g).astype(jnp.bfloat16)
+        grad_inner_g = times_t(mlp_grad_group, down_part)
+        grad_gate_g = (grad_inner_g * up_g * sig_g * (1.0 + gate_g * (1.0 - sig_g))).astype(
+            jnp.bfloat16
+        )
+        grad_up_g = (grad_inner_g * gate_g * sig_g).astype(jnp.bfloat16)
+        sum_down = scatter_join(split_cols(t_times(inner_g, mlp_grad_group), inner_count), inner_count, 0)
+        sum_gate = scatter_join(split_rows(t_times(hidden_group, grad_gate_g), inner_count), inner_count, 1)
+        sum_up = scatter_join(split_rows(t_times(hidden_group, grad_up_g), inner_count), inner_count, 1)
     grad_hidden = grad_output + lax.psum_scatter(
         (times_t(grad_gate_low, w_gate) + times_t(grad_up_low, w_up)).astype(jnp.bfloat16),
         "tensor",
@@ -279,7 +547,6 @@
     ).astype(jnp.float32)
     grad_attn, grad_gain_attn_part = post_norm_back(grad_hidden, a_unit, a_inv, gain_attn)
     attn_grad_all = lax.all_gather(grad_attn.astype(jnp.bfloat16), "tensor", axis=0, tiled=True)
-    grad_w_out = t_times(mixed_low, attn_grad_all)
     grad_mixed = times_t(attn_grad_all, w_out).astype(jnp.bfloat16)
     grad_q_rot, grad_k_rot, grad_values_low = jax.vmap(lambda *a: attend_back(a))(
         queries_low, keys_low, values_heads, segment, log_total, to_heads(grad_mixed)
@@ -300,9 +567,6 @@
         jnp.bfloat16
     )
     grad_values_flat = grad_values_low.reshape(row_count, local_width)
-    grad_w_query = t_times(gathered, grad_queries_low)
-    grad_w_key = t_times(gathered, grad_keys_low)
-    grad_w_value = t_times(gathered, grad_values_flat)
     grad_tokens = (
         grad_hidden
         + lax.psum_scatter(
@@ -324,15 +588,44 @@
     gain_total = lax.psum(gain_stack, ("dp", "tensor"))
     grad_gain_query = lax.dynamic_slice(gain_total[0], (tensor_start,), (local_width,))
     grad_gain_key = lax.dynamic_slice(gain_total[1], (tensor_start,), (local_width,))
-    summed = (
-        scatter_sum(split_rows(grad_w_query, inner_count), inner_count),
-        scatter_sum(split_rows(grad_w_key, inner_count), inner_count),
-        scatter_sum(split_rows(grad_w_value, inner_count), inner_count),
-        scatter_sum(split_cols(grad_w_out, inner_count), inner_count),
-        sum_gate,
-        sum_up,
-        sum_down,
-    )
+    if fused:
+        blocks, _, _ = weight_grads(
+            hidden_low,
+            grad_mlp_low,
+            hidden_all,
+            mlp_grad_all,
+            w_gate,
+            w_up,
+            w_down,
+            gathered,
+            attn_grad_all,
+            grad_queries_low,
+            grad_keys_low,
+            grad_values_flat,
+            mixed_low,
+        )
+        summed_attn = jnp.sum(blocks[:4].astype(jnp.float32), axis=1)
+        joined = blocks[4:].astype(jnp.float32)
+        width = joined.shape[3]
+        summed = (
+            summed_attn[1].T,
+            summed_attn[2].T,
+            summed_attn[0].T,
+            summed_attn[3],
+            joined[1].transpose(2, 0, 1).reshape(width, -1),
+            joined[2].transpose(2, 0, 1).reshape(width, -1),
+            joined[0].reshape(-1, width),
+        )
+    else:
+        summed = (
+            scatter_sum(split_rows(t_times(gathered, grad_queries_low), inner_count), inner_count),
+            scatter_sum(split_rows(t_times(gathered, grad_keys_low), inner_count), inner_count),
+            scatter_sum(split_rows(t_times(gathered, grad_values_flat), inner_count), inner_count),
+            scatter_sum(split_cols(t_times(mixed_low, attn_grad_all), inner_count), inner_count),
+            sum_gate,
+            sum_up,
+            sum_down,
+        )
     return (
         output,
         grad_tokens,

time: 898 us -> 674 us (0.75)
  Pallas kernels: 0 us -> 248 us
  waiting for transfers between devices: 382 us -> 184 us
  local copies, waits for them, and re-layouts: 124 us -> 40.2 us
  starting transfers between devices: 72.1 us -> 1.12 us
  matrix products: 149 us -> 84.7 us
  blocking collectives: 84.9 us -> 56.2 us
  other arithmetic: 56.6 us -> 39.4 us
    pallas_call x0 -> x1, Pallas kernels: none -> 248 us  [weight_grads(): pl.pallas_call(grads_kernel, name='weight_grads', out_shape=(jax.ShapeDty...]
    all_gather x4 -> x0, waiting for transfers between devices: 107 us -> none  [the longest x2 58.4 us: gather_group(): return lax.all_gather(part, 'tensor', axis=0, tiled=True)]
    ppermute x28 -> x0, waiting for transfers between devices: 86.7 us -> none  [swap(): return lax.ppermute(value, 'dp', [(d, d ^ shift) for d in range(size)])]
    ppermute x28 -> x0, starting transfers between devices: 71.1 us -> none  [swap(): return lax.ppermute(value, 'dp', [(d, d ^ shift) for d in range(size)])]
    dot_general x9 -> x0, matrix products: 55.6 us -> none  [the longest x7 36.4 us: t_times(): lax.dot_general(left_mat, right_mat, (((0,), (0,)), ((), ())), preferred_...]
    another operation x12 -> x0, local copies, waits for them, and re-layouts: 42.2 us -> none
    psum x1, blocking collectives: 72.5 us -> 43.7 us  [body(): gain_total = lax.psum(gain_stack, ('dp', 'tensor'))]
    reshape x4, local copies, waits for them, and re-layouts: 27.1 us -> 9.14 us  [the longest x2 5.05 us: to_heads(): return values.reshape(rows_dev, ROW_LEN, head_count, HD)]
  transfers between devices with their start and end apart: 40 -> 8, of which waited for: 18 -> 7; matrix products, arithmetic and copies ran while one was open for 23% -> 4% of each run, Pallas kernels for 0% -> 37%
where the time goes in v2:
time: 674 us; the launch traced here: 669 us
  Pallas kernels  248 us (37%)
  waiting for transfers between devices  184 us (27%)
  matrix products  84.7 us (13%)
  blocking collectives  56.2 us (8%)
  local copies, waits for them, and re-layouts  40.2 us (6%)
  other arithmetic  39.4 us (6%)
  between operations  15 us (2%)
    pallas_call x1, Pallas kernels, weight_grads(): pl.pallas_call(grads_kernel, name='weight_grads', out_shape=(jax.ShapeDty...  248 us
    psum x1, blocking collectives, body(): gain_total = lax.psum(gain_stack, ('dp', 'tensor'))  43.7 us
    dot_general x7, matrix products, times_t(): lax.dot_general(left_mat, right_mat, (((1,), (1,)), ((), ())), preferred_...  41.9 us
    reduce_scatter x1, waiting for transfers between devices, body(): lax.psum_scatter(jnp.dot(mixed_low, w_out, preferred_element_type=jnp.flo...  32.6 us
    reduce_scatter x1, waiting for transfers between devices, body(): lax.psum_scatter((times_t(grad_gate_low, w_gate) + times_t(grad_up_low, w...  31.6 us
    reduce_scatter x1, waiting for transfers between devices, body(): lax.psum_scatter(jnp.dot(inner_low, w_down, preferred_element_type=jnp.fl...  31.5 us
    all_gather x1, waiting for transfers between devices, body(): gathered = lax.all_gather(tokens, 'tensor', axis=0, tiled=True)  22.7 us
    all_gather x1, waiting for transfers between devices, body(): hidden_all = lax.all_gather(hidden_low, 'tensor', axis=0, tiled=True)  22.5 us
  transfers between devices with their start and end apart: 8, of which 7 were waited for; matrix products, arithmetic and copies ran while one was open for 4% of the time, Pallas kernels for 37%

profile of v2, /device:TPU:0, one launch (start us, length us, event | category | flops | bytes accessed | tf_op | source)
XLA Modules:
  0.0 669.4 jit_solution(9909995048642000211)
XLA Ops:
  10.4 1.8 broadcast_multiply_fusion
  12.2 22.7 %all-gather.5.cloned.1.call-done.tok_ref = bf16[512,2048]{1,0:T(8,128)(2,1)} async-done(((bf16[128,2048]{1,0:T(8,128)(2,1)}), bf16[512,2048]{1,0:T(8,128)(2,1)}) %all-gather.5.cloned.1.call-update) | async-done | bytes 2097168 | tf_op jit(solution)/shard_map/all_gather | solution.py:455
  34.9 3.5 multiply_reduce_fusion.4
  38.4 1.3 copy.52
  39.8 3.9 multiply_reduce_fusion.3
  43.6 1.6 copy.55
  45.2 6.4 all-reduce.1
  51.6 1.1 multiply_multiply_fusion
  52.8 2.5 reshape.517
  55.3 2.3 multiply_multiply_fusion.1
  57.6 2.5 reshape.516
  60.2 2.3 fusion.52
  64.0 1.4 fusion.55
  66.1 1.1 copy-done.33
  67.2 1.3 convolution_convert_fusion.3
  68.5 0.9 fusion.21
  70.3 2.6 convolution_convert_fusion.1
  73.0 32.6 %reduce-scatter.5.cloned.1.call-done = bf16[128,2048]{1,0:T(8,128)(2,1)} async-done(((bf16[512,2048]{1,0:T(8,128)(2,1)}), bf16[128,2048]{1,0:T(8,128)(2,1)}) %reduce-scatter.5.cloned.1.call-update) | async-done | bytes 524304 | tf_op jit(solution)/shard_map/reduce_scatter | solution.py:479
  105.6 1.2 fusion.31
  106.8 2.3 fusion.40.hid_ref
  109.3 22.5 %all-gather.7.cloned.1.call-done.hall_ref = bf16[512,2048]{1,0:T(8,128)(2,1)} async-done(((bf16[128,2048]{1,0:T(8,128)(2,1)}), bf16[512,2048]{1,0:T(8,128)(2,1)}) %all-gather.7.cloned.1.call-update) | async-done | bytes 2097168 | tf_op jit(solution)/shard_map/all_gather | solution.py:489
  131.9 8.5 %fusion.56 = f32[512,2048]{1,0:T(8,128)S(1)} fusion(bf16[512,2048]{1,0:T(8,128)(2,1)} %all-gather.7.cloned.1.call-done.hall_ref, bf16[2048,2048]{1,0:T(8,128)(2,1)} %wg_ref.1), kind=kOutput, calls=%fused_computation.134 | convolution fusion | flops 4294967296 | bytes 14680064 | tf_op jit(solution)/shard_map/dot_general | solution.py:501
  140.5 8.4 %fusion.57 = f32[512,2048]{1,0:T(8,128)S(1)} fusion(bf16[512,2048]{1,0:T(8,128)(2,1)S(1)} %copy-done.34, bf16[2048,2048]{1,0:T(8,128)(2,1)} %wu_ref.1), kind=kOutput, calls=%fused_computation.135 | convolution fusion | flops 4294967296 | bytes 14680064 | tf_op jit(solution)/shard_map/dot_general | solution.py:502
  148.9 2.0 copy-done.36
  150.9 5.8 convolution_convert_fusion
  156.8 31.5 %reduce-scatter.7.cloned.1.call-done = bf16[128,2048]{1,0:T(8,128)(2,1)} async-done(((bf16[512,2048]{1,0:T(8,128)(2,1)}), bf16[128,2048]{1,0:T(8,128)(2,1)}) %reduce-scatter.7.cloned.1.call-update) | async-done | bytes 524304 | tf_op jit(solution)/shard_map/reduce_scatter | solution.py:505
  188.4 1.2 fusion.35
  189.6 1.6 fusion.36
  191.2 2.4 fusion.24.dml_ref
  193.9 22.5 %all-gather.9.cloned.1.call-done.dall_ref = bf16[512,2048]{1,0:T(8,128)(2,1)} async-done(((bf16[128,2048]{1,0:T(8,128)(2,1)}), bf16[512,2048]{1,0:T(8,128)(2,1)}) %all-gather.9.cloned.1.call-update) | async-done | bytes 2097168 | tf_op jit(solution)/shard_map/all_gather | solution.py:517
  216.4 7.6 %fusion.58 = f32[512,2048]{1,0:T(8,128)S(1)} fusion(bf16[512,2048]{1,0:T(8,128)(2,1)} %all-gather.9.cloned.1.call-done.dall_ref, bf16[2048,2048]{1,0:T(8,128)(2,1)} %wd_ref.1), kind=kOutput, calls=%fused_computation.136 | convolution fusion | flops 4294967296 | bytes 14680064 | tf_op jit(solution)/shard_map/dot_general | solution.py:55
  224.0 13.6 %fusion.7 = f32[512,2048]{1,0:T(8,128)} fusion(bf16[2048,2048]{1,0:T(8,128)(2,1)} %wg_ref.1, f32[512,2048]{1,0:T(8,128)} %copy-done.35, f32[512,2048]{1,0:T(8,128)S(1)} %fusion.58, f32[512,2048]{1,0:T(8,128)} %copy-done.36), kind=kOutput, calls=%fused_computation.22 | convolution fusion | flops 4305453056 | bytes 25165824 | tf_op jit(solution)/shard_map/dot_general | solution.py:55
  237.6 11.7 %add_convert_fusion.1 = bf16[512,2048]{1,0:T(8,128)(2,1)} fusion(f32[512,2048]{1,0:T(8,128)} %fusion.7, bf16[2048,2048]{1,0:T(8,128)(2,1)} %wu_ref.1, f32[512,2048]{1,0:T(8,128)S(1)} %fusion.58, f32[512,2048]{1,0:T(8,128)} %copy-done.35), kind=kOutput, calls=%fused_computation.5 | convolution fusion | flops 4303355904 | bytes 23068672 | tf_op jit(solution)/shard_map/dot_general | solution.py:55
  249.4 31.6 %reduce-scatter.9.cloned.1.call-done = bf16[128,2048]{1,0:T(8,128)(2,1)} async-done(((bf16[512,2048]{1,0:T(8,128)(2,1)}), bf16[128,2048]{1,0:T(8,128)(2,1)}) %reduce-scatter.9.cloned.1.call-update) | async-done | bytes 524304 | tf_op jit(solution)/shard_map/reduce_scatter | solution.py:542
  281.0 1.8 fusion.30
  282.8 3.3 fusion.29
  286.5 2.1 copy.87.mix_ref
  288.6 20.2 %all-gather.11.cloned.1.call-done.dat_ref = bf16[512,2048]{1,0:T(8,128)(2,1)} async-done(((bf16[128,2048]{1,0:T(8,128)(2,1)}), bf16[512,2048]{1,0:T(8,128)(2,1)}) %all-gather.11.cloned.1.call-update) | async-done | bytes 2097168 | tf_op jit(solution)/shard_map/all_gather | solution.py:549
  308.8 3.6 convolution_convert_fusion.2
  312.5 1.6 fusion.18
  314.2 1.0 multiply_reduce_fusion
  315.1 1.2 multiply_convert_fusion
  316.4 1.8 fusion.9
  318.2 2.0 fusion.10
  320.2 2.0 copy.88.dv_ref
  322.2 2.9 multiply_subtract_fusion
  328.6 6.0 all-reduce
  334.6 1.8 multiply_convert_fusion.8.dq_ref
  336.4 1.7 multiply_convert_fusion.7.dk_ref
  338.1 1.3 fusion.60
  339.9 1.3 fusion.59
  341.7 2.7 add_convert_fusion
  344.4 248.4 %weight_grads.1 = (bf16[7,4,512,256]{3,2,1,0:T(8,128)(2,1)}, bf16[4,4,128,2048]{3,2,1,0:T(8,128)(2,1)}, bf16[4,4,128,2048]{3,2,1,0:T(8,128)(2,1)}) custom-call(bf16[128,2048]{1,0:T(8,128)(2,1)} %fusion.40.hid_ref, bf16[128,2048]{1,0:T(8,128)(2,1)} %fusion.24.dml_ref, bf16[512,2048]{1,0:T(8,128)(2,1)} %all-gather.7.cloned.1.call-done.hall_ref, ...), custom_call_target="tpu_custom_call" | custom-call | flops 30064771072 | bytes 62914560 | tf_op jit(solution)/shard_map/weight_grads/pallas_call | solution.py:395
  592.8 2.5 slice_convert_fusion
  595.3 2.9 fusion.51
  598.3 2.9 copy.76
  601.2 3.1 convert_reduce_fusion
  604.2 1.3 slice_bitcast_fusion
  605.6 2.1 copy.74
  607.7 2.0 copy.73
  609.7 2.0 copy.72
  611.8 2.9 copy.75
  614.7 43.7 %psum.39 = f32[4,2048]{1,0:T(4,128)S(1)} all-reduce(f32[4,2048]{1,0:T(4,128)S(1)} %pad_maximum_fusion.8), channel_id=1, replica_groups=mesh['dp'=8,'tensor'=4] {'dp','tensor'}, use_global_device_ids=true, to_apply=%region_27.28 | all-reduce | flops 8192 | bytes 65536 | tf_op jit(solution)/shard_map/psum | solution.py:588
  660.3 2.1 add_convert_fusion.2
  (124 shorter events, 13.6 us)
Async XLA Ops:
  7.2 32.6 %copy-start = (bf16[2048,512]{1,0:T(8,128)(2,1)S(1)}, bf16[2048,512]{1,0:T(8,128)(2,1)}, u32[]{:S(2)}) copy-start(bf16[2048,512]{1,0:T(8,128)(2,1)} %param.17) | copy-start | bytes 6291460
  7.2 27.7 %all-gather.5.cloned.1.call-start = ((), (), s32[]{:S(2)}) async-start(), calls=%async_computation.4 | async-start | bytes 2621440 | tf_op jit(solution)/shard_map/all_gather | solution.py:455
  7.9 97.7 %reduce-scatter.5.cloned.1.call-start = ((), (), s32[]{:S(2)}) async-start(), calls=%async_computation.5 | async-start | bytes 2621440 | tf_op jit(solution)/shard_map/reduce_scatter | solution.py:479
  39.7 11.9 %copy-start.31 = (f32[512]{0:T(512)S(1)}, f32[512]{0:T(512)}, u32[]{:S(2)}) copy-start(f32[512]{0:T(512)} %param.24) | copy-start | bytes 6148
  43.6 11.7 %copy-start.30 = (f32[512]{0:T(512)S(1)}, f32[512]{0:T(512)}, u32[]{:S(2)}) copy-start(f32[512]{0:T(512)} %param.23) | copy-start | bytes 6148
  60.2 2.3 copy-start.7
  60.2 2.9 copy-start.24
  63.1 1.0 copy-start.23
  63.7 2.4 copy-start.10
  63.7 2.4 copy-start.12
  63.7 2.4 copy-start.14
  63.7 2.4 copy-start.16
  64.0 2.0 copy-start.20
  64.0 3.2 copy-start.33
  65.4 3.1 copy-start.1
  68.5 1.0 copy-start.25
  68.5 1.8 copy-start.32
  69.5 0.8 copy-start.27
  70.3 36.5 %copy-start.28 = (f32[2048]{0:T(1024)S(1)}, f32[2048]{0:T(1024)}, u32[]{:S(2)}) copy-start(f32[2048]{0:T(1024)} %param.25) | copy-start | bytes 24580
  72.9 59.0 %all-gather.7.cloned.1.call-start = ((), (), s32[]{:S(2)}) async-start(), calls=%async_computation.6 | async-start | bytes 2621440 | tf_op jit(solution)/shard_map/all_gather | solution.py:489
  109.1 79.2 %reduce-scatter.7.cloned.1.call-start = ((), (), s32[]{:S(2)}) async-start(), calls=%async_computation.7 | async-start | bytes 2621440 | tf_op jit(solution)/shard_map/reduce_scatter | solution.py:505
  131.9 8.5 %copy-start.34 = (bf16[512,2048]{1,0:T(8,128)(2,1)S(1)}, bf16[512,2048]{1,0:T(8,128)(2,1)}, u32[]{:S(2)}) copy-start(bf16[512,2048]{1,0:T(8,128)(2,1)} %all-gather.7.cloned.1.call-done.hall_ref) | copy-start | bytes 6291460
  131.9 19.0 %slice-start = ((s8[8388608]{0:T(1024)(128)(4,1)}), s8[4194304]{0:T(1024)(128)(4,1)S(1)}, s32[]{:S(2)}) async-start(s8[8388608]{0:T(1024)(128)(4,1)} %bitcast.140), calls=%async_computation.12 | async-start | bytes 8388608
  140.4 8.5 %copy-start.35 = (f32[512,2048]{1,0:T(8,128)}, f32[512,2048]{1,0:T(8,128)S(1)}, u32[]{:S(2)}) copy-start(f32[512,2048]{1,0:T(8,128)S(1)} %fusion.56) | copy-start | bytes 12582916
  140.4 10.4 %slice-start.1 = ((s8[8388608]{0:T(1024)(128)(4,1)}), s8[4194304]{0:T(1024)(128)(4,1)S(1)}, s32[]{:S(2)}) async-start(s8[8388608]{0:T(1024)(128)(4,1)} %bitcast.140), calls=%async_computation.13 | async-start | bytes 8388608
  148.9 2.0 copy-start.36
  150.9 38.7 %copy-start.29 = (f32[2048]{0:T(1024)S(1)}, f32[2048]{0:T(1024)}, u32[]{:S(2)}) copy-start(f32[2048]{0:T(1024)} %param.26) | copy-start | bytes 24580
  156.8 59.6 %all-gather.9.cloned.1.call-start = ((), (), s32[]{:S(2)}) async-start(), calls=%async_computation.8 | async-start | bytes 2621440 | tf_op jit(solution)/shard_map/all_gather | solution.py:517
  193.6 87.3 %reduce-scatter.9.cloned.1.call-start = ((), (), s32[]{:S(2)}) async-start(), calls=%async_computation.9 | async-start | bytes 2621440 | tf_op jit(solution)/shard_map/reduce_scatter | solution.py:542
  249.4 59.5 %all-gather.11.cloned.1.call-start = ((), (), s32[]{:S(2)}) async-start(), calls=%async_computation.10 | async-start | bytes 2621440 | tf_op jit(solution)/shard_map/all_gather | solution.py:549
  286.1 374.2 %reduce-scatter.11.cloned.1.call-start = ((), (), s32[]{:S(2)}) async-start(), calls=%async_computation.11 | async-start | bytes 2621440 | tf_op jit(solution)/shard_map/reduce_scatter | solution.py:572
  308.8 3.7 copy-start.2
  312.5 1.7 copy-start.26
  315.1 1.2 copy-start.15
  315.1 1.2 copy-start.17
  316.4 1.8 copy-start.11
  316.4 1.8 copy-start.13
  326.2 2.0 copy-start.5
  326.2 1.6 copy-start.3
  327.6 1.0 copy-start.6
  336.4 3.0 copy-start.18
  338.1 1.3 copy-start.19
  338.1 1.8 copy-start.22
  339.9 1.3 copy-start.8
  339.9 1.8 copy-start.21
  605.6 54.7 %copy-start.4 = (bf16[128,2048]{1,0:T(8,128)(2,1)S(1)}, bf16[128,2048]{1,0:T(8,128)(2,1)}, u32[]{:S(2)}) copy-start(bf16[128,2048]{1,0:T(8,128)(2,1)} %param.27) | copy-start | bytes 1572868
  605.6 54.7 %copy-start.9 = (bf16[128,2048]{1,0:T(8,128)(2,1)S(1)}, bf16[128,2048]{1,0:T(8,128)(2,1)}, u32[]{:S(2)}) copy-start(bf16[128,2048]{1,0:T(8,128)(2,1)} %reduce-scatter.9.cloned.1.call-done) | copy-start | bytes 1572868
Sparse Core Ops, SparseCore 0:
  9.6 25.2 all-gather.4
  73.1 32.5 reduce-scatter.4
  109.2 22.5 all-gather.6
  156.9 31.4 reduce-scatter.6
  193.8 22.5 all-gather.8
  249.5 31.4 reduce-scatter.8
  286.2 22.5 all-gather.10
  344.5 39.6 reduce-scatter.10

commit v3 on v2

--- a/solution.py
+++ b/solution.py
@@ -175,7 +175,7 @@
 
 
 def grads_kernel(
-    hid_ref, dml_ref, hall_ref, dall_ref, wg_ref, wu_ref, wd_ref, tok_ref, dat_ref, dq_ref, dk_ref, dv_ref, mix_ref,
+    dml_ref, gh_in, gm_in, wg_ref, wu_ref, wd_ref, tok_ref, dat_ref, dq_ref, dk_ref, dv_ref, mix_ref,
     out_ref, gh_ref, gm_ref,
     rows_v, wg_v, wu_v, wd_v, lhs_in, lhs_t, acc, full, part,
     ld_sem, zs_s, zs_r, xs_s, xs_r, cs_s, cs_r, ys_s, ys_r, ts_s, ts_r, own_s,
@@ -205,8 +205,8 @@
         pltpu.make_async_copy(dq_ref, lhs_in.at[1], ld_sem.at[3]),
         pltpu.make_async_copy(dk_ref, lhs_in.at[2], ld_sem.at[4]),
         pltpu.make_async_copy(mix_ref, lhs_in.at[3], ld_sem.at[5]),
-        pltpu.make_async_copy(hall_ref, rows_v.at[0, 0], ld_sem.at[6]),
-        pltpu.make_async_copy(dall_ref, rows_v.at[0, 1], ld_sem.at[7]),
+        pltpu.make_async_copy(gh_ref.at[z], rows_v.at[0, 0], ld_sem.at[6]),
+        pltpu.make_async_copy(gm_ref.at[z], rows_v.at[0, 1], ld_sem.at[7]),
         pltpu.make_async_copy(wg_ref.at[:, pl.ds(z * f, f)], wg_v, ld_sem.at[8]),
         pltpu.make_async_copy(wu_ref.at[:, pl.ds(z * f, f)], wu_v, ld_sem.at[9]),
         pltpu.make_async_copy(wd_ref.at[pl.ds(z * f, f), :], wd_v, ld_sem.at[10]),
@@ -219,11 +219,10 @@
         pl.semaphore_signal(barrier, inc=1, device_id=(dd, tt), device_id_type=MESH)
     pl.semaphore_wait(barrier, 6)
 
-    shards = (hid_ref, dml_ref)
     groups = (gh_ref, gm_ref)
 
-    def gather_z(a, k):
-        return remote(shards[a], groups[a].at[z, t], zs_s.at[a, k - 1], zs_r.at[a, k - 1], peer(k), t)
+    def gather_z(k):
+        return remote(dml_ref, gm_ref.at[z, t], zs_s.at[k - 1], zs_r.at[k - 1], peer(k), t)
 
     def forward_x(a, k):
         r = (z + 4 - k) % 4
@@ -236,8 +235,8 @@
 
     order = (1, 3, 2)
     for k in order:
-        for a in range(2):
-            gather_z(a, k).start()
+        forward_x(0, k).start()
+        gather_z(k).start()
 
     def swap_y(w):
         return remote(full.at[w, :, 1 - y], part.at[w], ys_s.at[w], ys_r.at[w], twin, t)
@@ -268,7 +267,7 @@
         def tile(j, carry):
             cols = pl.ds(pl.multiple_of(j * width, width), width)
             full[w, j // 2, j % 2] = jnp.dot(
-                lhs_t[0], rows_v[1, side, :, cols], preferred_element_type=jnp.float32
+                lhs_t[0], rows_v[1, side, :, :, cols].reshape(lhs_t.shape[2], width), preferred_element_type=jnp.float32
             ).astype(jnp.bfloat16)
             return carry
 
@@ -284,14 +283,15 @@
         attn_grad(w, 0)
 
     step = 256
+    tall = (lhs_t.shape[2], acc.shape[2])
 
     def mlp_row(slot, first):
         def wide(j, carry):
             cols = pl.ds(pl.multiple_of(j * step, step), step)
-            g = jnp.dot(rows_v[slot, 0], wg_v[:, cols], preferred_element_type=jnp.float32)
-            u = jnp.dot(rows_v[slot, 0], wu_v[:, cols], preferred_element_type=jnp.float32)
+            g = jnp.dot(rows_v[slot, 0].reshape(tall), wg_v[:, cols], preferred_element_type=jnp.float32)
+            u = jnp.dot(rows_v[slot, 0].reshape(tall), wu_v[:, cols], preferred_element_type=jnp.float32)
             di = lax.dot_general(
-                rows_v[slot, 1], wd_v[cols, :], (((1,), (1,)), ((), ())), preferred_element_type=jnp.float32
+                rows_v[slot, 1].reshape(tall), wd_v[cols, :], (((1,), (1,)), ((), ())), preferred_element_type=jnp.float32
             )
             sg = jax.nn.sigmoid(g)
             gs = g * sg
@@ -305,7 +305,7 @@
         def deep(j, carry):
             cols = pl.ds(pl.multiple_of(j * step, step), step)
             for w, side in ((0, 1), (1, 0), (2, 0)):
-                new = jnp.dot(lhs_t[w], rows_v[slot, side, :, cols], preferred_element_type=jnp.float32)
+                new = jnp.dot(lhs_t[w], rows_v[slot, side, :, :, cols].reshape(lhs_t.shape[2], step), preferred_element_type=jnp.float32)
                 if first:
                     acc[w, :, cols] = new
                 else:
@@ -319,9 +319,8 @@
     mlp_row(0, True)
 
     def advance_x(k):
-        for a in range(2):
-            gather_z(a, k).wait_recv()
-            forward_x(a, k).start()
+        gather_z(k).wait_recv()
+        forward_x(1, k).start()
 
     def advance_c(k):
         for a in range(2):
@@ -332,7 +331,7 @@
     def row_loads(k, slot):
         r = (z + 4 - k) % 4
         return [
-            pltpu.make_async_copy(groups[a].at[r, q], rows_v.at[slot, a, pl.ds(q * 128, 128)], ld_sem.at[a * 4 + q])
+            pltpu.make_async_copy(groups[a].at[r, q], rows_v.at[slot, a, q], ld_sem.at[a * 4 + q])
             for a in range(2)
             for q in range(4)
         ]
@@ -374,8 +373,8 @@
     for w in range(3):
         finish_y(4 + w)
     for k in order:
+        gather_z(k).wait_send()
         for a in range(2):
-            gather_z(a, k).wait_send()
             forward_x(a, k).wait_send()
             for h in range(2):
                 forward_c(a, k, h).wait_send()
@@ -385,8 +384,10 @@
             trade_z(w, k).wait()
 
 
-def weight_grads(hid, dml, hall, dall, wg, wu, wd, tok, dat, dq, dk, dv, mix):
-    rows, width = hall.shape
+def weight_grads(dml, gh, gd, wg, wu, wd, tok, dat, dq, dk, dv, mix):
+    rows, width = tok.shape
+    tok = tok.reshape(4, rows // 4, width)
+    dat = dat.reshape(4, rows // 4, width)
     f = wg.shape[1] // 4
     block = width // 8
     bf = jnp.bfloat16
@@ -395,15 +396,16 @@
     return pl.pallas_call(
         grads_kernel,
         name="weight_grads",
+        input_output_aliases={1: 1, 2: 2},
         out_shape=(
             jax.ShapeDtypeStruct((7, 4, f, block), bf),
             jax.ShapeDtypeStruct((4, 4, rows // 4, width), bf),
             jax.ShapeDtypeStruct((4, 4, rows // 4, width), bf),
         ),
-        in_specs=[FULL] * 13,
+        in_specs=[FULL] * 12,
         out_specs=(FULL,) * 3,
         scratch_shapes=[
-            pltpu.VMEM((2, 2, rows, width), bf),
+            pltpu.VMEM((2, 2, 4, rows // 4, width), bf),
             pltpu.VMEM((width, f), bf),
             pltpu.VMEM((width, f), bf),
             pltpu.VMEM((f, width), bf),
@@ -413,8 +415,8 @@
             pltpu.VMEM((7, 4, 2, f, block), bf),
             pltpu.VMEM((7, 4, f, block), bf),
             dma((11,)),
-            dma((2, 3)),
-            dma((2, 3)),
+            dma((3,)),
+            dma((3,)),
             dma((2, 3)),
             dma((2, 3)),
             dma((2, 3, 2)),
@@ -429,7 +431,265 @@
             collective_id=0, has_side_effects=True, vmem_limit_bytes=60 * 1024 * 1024
         ),
         cost_estimate=pl.CostEstimate(flops=flops, bytes_accessed=60 * 1024 * 1024, transcendentals=0),
-    )(hid, dml, hall, dall, wg, wu, wd, tok, dat, dq, dk, dv, mix)
+    )(dml, gh, gd, wg, wu, wd, tok, dat, dq, dk, dv, mix)
+
+
+def far_copy(src, dst, ss, rs, dd, tt):
+    return pltpu.make_async_remote_copy(
+        src_ref=src, dst_ref=dst, send_sem=ss, recv_sem=rs, device_id=(dd, tt), device_id_type=MESH
+    )
+
+
+def mean_inv(values):
+    return lax.rsqrt(jnp.mean(values * values, axis=1, keepdims=True) + EPS)
+
+
+def mlp_kernel(
+    att_ref, tok_ref, cot_ref, ga_ref, gm_ref, wg_ref, wu_ref, wd_ref,
+    out_ref, ghid_ref, dat_ref, dml_ref, gain_ref, gh_ref, gd_ref,
+    wg_v, wu_v, wd_v, slope_g, slope_u, own, oth, low_a, low_b, pown, pmate, xsend, xrecv, qown, qmate, hid,
+    w_sem, as_s, as_r, ax_s, ax_r, af_s, af_r, ps_s, ps_r, px_s, px_r, pq_s, pq_r, zs_s, zs_r, st_sem,
+):
+    d = lax.axis_index("dp")
+    t = lax.axis_index("tensor")
+    z = d // 2
+    y = d % 2
+    c = t % 2
+    chip = t // 2
+    mate = t + 1 - 2 * c
+    across = (t + 2) % 4
+    shard, width = att_ref.shape
+    ff = wg_v.shape[1]
+    bf = jnp.bfloat16
+    f32 = jnp.float32
+    tile = 512
+    tiles = ff // tile
+
+    def wcopy(i, j):
+        cols = pl.ds(j * tile, tile)
+        if i == 0:
+            return pltpu.make_async_copy(wg_ref.at[:, cols], wg_v.at[:, cols], w_sem.at[0, j])
+        if i == 1:
+            return pltpu.make_async_copy(wu_ref.at[:, cols], wu_v.at[:, cols], w_sem.at[1, j])
+        return pltpu.make_async_copy(wd_ref.at[cols, :], wd_v.at[cols, :], w_sem.at[2, j])
+
+    for j in range(tiles):
+        wcopy(0, j).start()
+        wcopy(1, j).start()
+    for j in range(tiles):
+        wcopy(2, j).start()
+
+    barrier = pltpu.get_barrier_semaphore()
+    peers = [((z + k) % 4) * 2 + y for k in range(1, 4)]
+    for dd, tt in [(peers[0], t), (peers[1], t), (peers[2], t), (d, mate), (d, across)]:
+        pl.semaphore_signal(barrier, inc=1, device_id=(dd, tt), device_id_type=MESH)
+    pl.semaphore_wait(barrier, 5)
+
+    def send_mate(p):
+        return far_copy(own.at[p, c], own.at[p, c], as_s.at[p], as_r.at[p], d, mate)
+
+    def send_across(p):
+        return far_copy(own.at[p, c], oth.at[p, c], ax_s.at[p], ax_r.at[p], d, across)
+
+    def forward(p):
+        return far_copy(oth.at[p, c], oth.at[p, c], af_s.at[p], af_r.at[p], d, mate)
+
+    half = width // 2
+
+    def part_mate(p, h):
+        return far_copy(
+            pown.at[p, h, 1 - c], pmate.at[p, h], ps_s.at[p, h], ps_r.at[p, h], d, mate
+        )
+
+    def part_across(p, h):
+        return far_copy(xsend.at[p, h], xrecv.at[p, h], px_s.at[p, h], px_r.at[p, h], d, across)
+
+    def part_own(p):
+        return far_copy(qown.at[p, 1 - c], qmate.at[p], pq_s.at[p], pq_r.at[p], d, mate)
+
+    def gather_z(k):
+        return far_copy(
+            own.at[0, c], gh_ref.at[z, t], zs_s.at[k - 1], zs_r.at[k - 1], ((z + k) % 4) * 2 + y, t
+        )
+
+    def store_row(p, ref):
+        mine = ref.at[z]
+        return [
+            pltpu.make_async_copy(own.at[p, 0], mine.at[chip * 2], st_sem.at[p, 0]),
+            pltpu.make_async_copy(own.at[p, 1], mine.at[chip * 2 + 1], st_sem.at[p, 1]),
+            pltpu.make_async_copy(oth.at[p, 0], mine.at[2 - chip * 2], st_sem.at[p, 2]),
+            pltpu.make_async_copy(oth.at[p, 1], mine.at[3 - chip * 2], st_sem.at[p, 3]),
+        ]
+
+    two = 2 * shard
+
+    def forward_in(lhs, base, wait):
+        for j in range(tiles):
+            if wait:
+                wcopy(0, j).wait()
+                wcopy(1, j).wait()
+            cols = pl.ds(j * tile, tile)
+            for s in range(2):
+                rows = pl.ds(s * shard, shard)
+                g = jnp.dot(lhs[s], wg_v[:, cols], preferred_element_type=f32)
+                u = jnp.dot(lhs[s], wu_v[:, cols], preferred_element_type=f32)
+                sg = jax.nn.sigmoid(g)
+                gs = g * sg
+                low_a[rows, cols] = (gs * u).astype(bf)
+                slope_u[pl.ds(base + s * shard, shard), cols] = gs
+                slope_g[pl.ds(base + s * shard, shard), cols] = u * sg * (1.0 + g * (1.0 - sg))
+
+    def backward_in(lhs, base, wait):
+        for j in range(tiles):
+            cols = pl.ds(j * tile, tile)
+            for s in range(2):
+                rows = pl.ds(s * shard, shard)
+                di = lax.dot_general(
+                    lhs[s], wd_v[cols, :], (((1,), (1,)), ((), ())), preferred_element_type=f32
+                )
+                low_a[rows, cols] = (di * slope_g[pl.ds(base + s * shard, shard), cols]).astype(bf)
+                low_b[rows, cols] = (di * slope_u[pl.ds(base + s * shard, shard), cols]).astype(bf)
+
+    def result(p, cols):
+        if p == 0:
+            return jnp.dot(low_a[...], wd_v[:, cols], preferred_element_type=f32)
+        nt = (((1,), (1,)), ((), ()))
+        return lax.dot_general(
+            low_a[...], wg_v[cols, :], nt, preferred_element_type=f32
+        ) + lax.dot_general(low_b[...], wu_v[cols, :], nt, preferred_element_type=f32)
+
+    def run(p, first, wait):
+        send_across(p).start()
+        send_mate(p).start()
+        if p == 0:
+            for k in (1, 3, 2):
+                gather_z(k).start()
+        send_mate(p).wait_recv()
+        first(own.at[p], 0, wait)
+        if wait:
+            for j in range(tiles):
+                wcopy(2, j).wait()
+        for j in range(width // tile):
+            cols = pl.ds(j * tile, tile)
+            new = result(p, cols).astype(bf)
+            for s in range(2):
+                qown[p, s, :, cols] = new[s * shard : (s + 1) * shard]
+        part_own(p).start()
+        send_across(p).wait_recv()
+        forward(p).start()
+        forward(p).wait_recv()
+        for cp in store_row(p, gh_ref if p == 0 else gd_ref):
+            cp.start()
+        first(oth.at[p], two, False)
+        for h in range(2):
+            for j in range(half // tile):
+                new = result(p, pl.ds(h * half + j * tile, tile)).astype(bf)
+                for s in range(2):
+                    pown[p, h, s, :, pl.ds(j * tile, tile)] = new[s * shard : (s + 1) * shard]
+            part_mate(p, h).start()
+            part_mate(p, h).wait_recv()
+            xsend[p, h] = (pown[p, h, c].astype(f32) + pmate[p, h].astype(f32)).astype(bf)
+            part_across(p, h).start()
+        part_own(p).wait_recv()
+        sums = []
+        for h in range(2):
+            part_across(p, h).wait_recv()
+            cols = slice(h * half, (h + 1) * half)
+            sums.append(
+                qown[p, c, :, cols].astype(f32) + qmate[p, :, cols].astype(f32) + xrecv[p, h].astype(f32)
+            )
+        return jnp.concatenate(sums, axis=1)
+
+    att = att_ref[...]
+    hid[...] = tok_ref[...].astype(f32) + att * mean_inv(att) * ga_ref[...]
+    own[0, c] = hid[...].astype(bf)
+    mlp = run(0, forward_in, True)
+    rf = mean_inv(mlp)
+    fh = mlp * rf
+    gy = cot_ref[...].astype(f32)
+    out_ref[...] = (hid[...] + fh * gm_ref[...]).astype(bf)
+    scaled = gy * gm_ref[...]
+    dm = (rf * (scaled - fh * jnp.mean(scaled * fh, axis=1, keepdims=True))).astype(bf)
+    gain_ref[1:2, :] = jnp.sum(gy * fh, axis=0, keepdims=True)
+    own[1, c] = dm
+    dml_ref[...] = dm
+    back = run(1, backward_in, False)
+    gh = cot_ref[...].astype(f32) + back
+    ghid_ref[...] = gh
+    ra = mean_inv(att_ref[...])
+    ah = att_ref[...] * ra
+    gain_ref[0:1, :] = jnp.sum(gh * ah, axis=0, keepdims=True)
+    scaled = gh * ga_ref[...]
+    dat_ref[...] = (ra * (scaled - ah * jnp.mean(scaled * ah, axis=1, keepdims=True))).astype(bf)
+
+    for p in range(2):
+        send_across(p).wait_send()
+        send_mate(p).wait_send()
+        forward(p).wait_send()
+        part_own(p).wait_send()
+        for h in range(2):
+            part_mate(p, h).wait_send()
+            part_across(p, h).wait_send()
+        for cp in store_row(p, gh_ref if p == 0 else gd_ref):
+            cp.wait()
+    for k in range(1, 4):
+        gather_z(k).wait()
+
+
+def mlp_both(att, tok, cot, ga, gm, wg, wu, wd):
+    shard, width = tok.shape
+    ff = wg.shape[1]
+    bf = jnp.bfloat16
+    f32 = jnp.float32
+    dma = pltpu.SemaphoreType.DMA
+    half = width // 2
+    vm = pl.BlockSpec(memory_space=pltpu.VMEM)
+    shape = jax.ShapeDtypeStruct
+    return pl.pallas_call(
+        mlp_kernel,
+        name="feed_forward",
+        out_shape=(
+            shape((shard, width), bf),
+            shape((shard, width), f32),
+            shape((shard, width), bf),
+            shape((shard, width), bf),
+            shape((2, width), f32),
+            shape((4, 4, shard, width), bf),
+            shape((4, 4, shard, width), bf),
+        ),
+        in_specs=[vm] * 5 + [FULL] * 3,
+        out_specs=(vm,) * 5 + (FULL,) * 2,
+        scratch_shapes=[
+            pltpu.VMEM((width, ff), bf),
+            pltpu.VMEM((width, ff), bf),
+            pltpu.VMEM((ff, width), bf),
+            pltpu.VMEM((4 * shard, ff), f32),
+            pltpu.VMEM((4 * shard, ff), f32),
+            pltpu.VMEM((2, 2, shard, width), bf),
+            pltpu.VMEM((2, 2, shard, width), bf),
+            pltpu.VMEM((2 * shard, ff), bf),
+            pltpu.VMEM((2 * shard, ff), bf),
+            pltpu.VMEM((2, 2, 2, shard, half), bf),
+            pltpu.VMEM((2, 2, shard, half), bf),
+            pltpu.VMEM((2, 2, shard, half), bf),
+            pltpu.VMEM((2, 2, shard, half), bf),
+            pltpu.VMEM((2, 2, shard, width), bf),
+            pltpu.VMEM((2, shard, width), bf),
+            pltpu.VMEM((shard, width), f32),
+            dma((3, ff // 512)),
+            dma((2,)), dma((2,)), dma((2,)), dma((2,)), dma((2,)), dma((2,)),
+            dma((2, 2)), dma((2, 2)), dma((2, 2)), dma((2, 2)),
+            dma((2,)), dma((2,)),
+            dma((3,)), dma((3,)),
+            dma((2, 4)),
+        ],
+        compiler_params=pltpu.CompilerParams(
+            collective_id=1, has_side_effects=True, vmem_limit_bytes=60 * 1024 * 1024
+        ),
+        cost_estimate=pl.CostEstimate(
+            flops=2 * 6 * 4 * shard * width * ff, bytes_accessed=40 * 1024 * 1024, transcendentals=4 * shard * ff
+        ),
+    )(att, tok, cot, ga.reshape(1, -1), gm.reshape(1, -1), wg, wu, wd)
 
 
 def body(
@@ -482,47 +742,50 @@
         scatter_dimension=0,
         tiled=True,
     ).astype(jnp.float32)
-    a_inv = lax.rsqrt(jnp.mean(attn_out * attn_out, axis=1, keepdims=True) + EPS)
-    a_unit = attn_out * a_inv
-    hidden = tokens.astype(jnp.float32) + a_unit * gain_attn
-    hidden_low = hidden.astype(jnp.bfloat16)
-    hidden_all = lax.all_gather(hidden_low, "tensor", axis=0, tiled=True)
+    fused = lax.axis_size("dp") == 8
     inner_count = lax.axis_size("dp") // OUTER
-    outer_index = lax.axis_index("dp") // inner_count
-
-    def gather_group(shard):
-        groups = [[z * inner_count + i for z in range(OUTER)] for i in range(inner_count)]
-        part = lax.all_gather(shard, "dp", axis=0, tiled=True, axis_index_groups=groups)
-        return lax.all_gather(part, "tensor", axis=0, tiled=True)
-
-    fused = lax.axis_size("dp") == 8
-    if not fused:
+    if fused:
+        output, grad_hidden, grad_attn_low, grad_mlp_low, gain_parts, group_h, group_d = mlp_both(
+            attn_out, tokens, cotangent, gain_attn, gain_mlp, w_gate, w_up, w_down
+        )
+        grad_gain_attn_part, grad_gain_mlp_part = gain_parts[0], gain_parts[1]
+    else:
+        a_inv = lax.rsqrt(jnp.mean(attn_out * attn_out, axis=1, keepdims=True) + EPS)
+        a_unit = attn_out * a_inv
+        hidden = tokens.astype(jnp.float32) + a_unit * gain_attn
+        hidden_low = hidden.astype(jnp.bfloat16)
+        hidden_all = lax.all_gather(hidden_low, "tensor", axis=0, tiled=True)
+        outer_index = lax.axis_index("dp") // inner_count
+
+        def gather_group(shard):
+            groups = [[z * inner_count + i for z in range(OUTER)] for i in range(inner_count)]
+            part = lax.all_gather(shard, "dp", axis=0, tiled=True, axis_index_groups=groups)
+            return lax.all_gather(part, "tensor", axis=0, tiled=True)
+
         hidden_group = gather_group(hidden_low)
-    gate_acts = jnp.dot(hidden_all, w_gate, preferred_element_type=jnp.float32)
-    up_acts = jnp.dot(hidden_all, w_up, preferred_element_type=jnp.float32)
-    gate_sigmoid = jax.nn.sigmoid(gate_acts)
-    inner_low = (gate_acts * gate_sigmoid * up_acts).astype(jnp.bfloat16)
-    mlp_out = lax.psum_scatter(
-        jnp.dot(inner_low, w_down, preferred_element_type=jnp.float32).astype(jnp.bfloat16),
-        "tensor",
-        scatter_dimension=0,
-        tiled=True,
-    ).astype(jnp.float32)
-    f_inv = lax.rsqrt(jnp.mean(mlp_out * mlp_out, axis=1, keepdims=True) + EPS)
-    f_unit = mlp_out * f_inv
-    output = (hidden + f_unit * gain_mlp).astype(jnp.bfloat16)
-    grad_output = cotangent.astype(jnp.float32)
-    grad_mlp, grad_gain_mlp_part = post_norm_back(grad_output, f_unit, f_inv, gain_mlp)
-    grad_mlp_low = grad_mlp.astype(jnp.bfloat16)
-    mlp_grad_all = lax.all_gather(grad_mlp_low, "tensor", axis=0, tiled=True)
-    if not fused:
+        gate_acts = jnp.dot(hidden_all, w_gate, preferred_element_type=jnp.float32)
+        up_acts = jnp.dot(hidden_all, w_up, preferred_element_type=jnp.float32)
+        gate_sigmoid = jax.nn.sigmoid(gate_acts)
+        inner_low = (gate_acts * gate_sigmoid * up_acts).astype(jnp.bfloat16)
+        mlp_out = lax.psum_scatter(
+            jnp.dot(inner_low, w_down, preferred_element_type=jnp.float32).astype(jnp.bfloat16),
+            "tensor",
+            scatter_dimension=0,
+            tiled=True,
+        ).astype(jnp.float32)
+        f_inv = lax.rsqrt(jnp.mean(mlp_out * mlp_out, axis=1, keepdims=True) + EPS)
+        f_unit = mlp_out * f_inv
+        output = (hidden + f_unit * gain_mlp).astype(jnp.bfloat16)
+        grad_output = cotangent.astype(jnp.float32)
+        grad_mlp, grad_gain_mlp_part = post_norm_back(grad_output, f_unit, f_inv, gain_mlp)
+        grad_mlp_low = grad_mlp.astype(jnp.bfloat16)
+        mlp_grad_all = lax.all_gather(grad_mlp_low, "tensor", axis=0, tiled=True)
         mlp_grad_group = gather_group(grad_mlp_low)
-    grad_inner = times_t(mlp_grad_all, w_down)
-    grad_gate_low = (
-        grad_inner * up_acts * gate_sigmoid * (1.0 + gate_acts * (1.0 - gate_sigmoid))
-    ).astype(jnp.bfloat16)
-    grad_up_low = (grad_inner * gate_acts * gate_sigmoid).astype(jnp.bfloat16)
-    if not fused:
+        grad_inner = times_t(mlp_grad_all, w_down)
+        grad_gate_low = (
+            grad_inner * up_acts * gate_sigmoid * (1.0 + gate_acts * (1.0 - gate_sigmoid))
+        ).astype(jnp.bfloat16)
+        grad_up_low = (grad_inner * gate_acts * gate_sigmoid).astype(jnp.bfloat16)
         part_width = w_gate.shape[1] // OUTER
         gate_part = lax.dynamic_slice_in_dim(w_gate, outer_index * part_width, part_width, 1)
         up_part = lax.dynamic_slice_in_dim(w_up, outer_index * part_width, part_width, 1)
@@ -539,14 +802,15 @@
         sum_down = scatter_join(split_cols(t_times(inner_g, mlp_grad_group), inner_count), inner_count, 0)
         sum_gate = scatter_join(split_rows(t_times(hidden_group, grad_gate_g), inner_count), inner_count, 1)
         sum_up = scatter_join(split_rows(t_times(hidden_group, grad_up_g), inner_count), inner_count, 1)
-    grad_hidden = grad_output + lax.psum_scatter(
-        (times_t(grad_gate_low, w_gate) + times_t(grad_up_low, w_up)).astype(jnp.bfloat16),
-        "tensor",
-        scatter_dimension=0,
-        tiled=True,
-    ).astype(jnp.float32)
-    grad_attn, grad_gain_attn_part = post_norm_back(grad_hidden, a_unit, a_inv, gain_attn)
-    attn_grad_all = lax.all_gather(grad_attn.astype(jnp.bfloat16), "tensor", axis=0, tiled=True)
+        grad_hidden = grad_output + lax.psum_scatter(
+            (times_t(grad_gate_low, w_gate) + times_t(grad_up_low, w_up)).astype(jnp.bfloat16),
+            "tensor",
+            scatter_dimension=0,
+            tiled=True,
+        ).astype(jnp.float32)
+        grad_attn, grad_gain_attn_part = post_norm_back(grad_hidden, a_unit, a_inv, gain_attn)
+        grad_attn_low = grad_attn.astype(jnp.bfloat16)
+    attn_grad_all = lax.all_gather(grad_attn_low, "tensor", axis=0, tiled=True)
     grad_mixed = times_t(attn_grad_all, w_out).astype(jnp.bfloat16)
     grad_q_rot, grad_k_rot, grad_values_low = jax.vmap(lambda *a: attend_back(a))(
         queries_low, keys_low, values_heads, segment, log_total, to_heads(grad_mixed)
@@ -590,10 +854,9 @@
     grad_gain_key = lax.dynamic_slice(gain_total[1], (tensor_start,), (local_width,))
     if fused:
         blocks, _, _ = weight_grads(
-            hidden_low,
             grad_mlp_low,
-            hidden_all,
-            mlp_grad_all,
+            group_h,
+            group_d,
             w_gate,
             w_up,
             w_down,

time: 674 us -> 535 us (0.79)
  waiting for transfers between devices: 184 us -> 74.4 us
  matrix products: 84.7 us -> 35.9 us
  Pallas kernels: 248 us -> 283 us
  other arithmetic: 39.4 us -> 23.9 us
    reduce_scatter x2 -> x0, waiting for transfers between devices: 63.1 us -> none  [the longest x1 31.6 us: body(): lax.psum_scatter((times_t(grad_gate_low, w_gate) + times_t(grad_up_low, w...]
    all_gather x3 -> x1, waiting for transfers between devices: 65.2 us -> 18.5 us  [body(): attn_grad_all = lax.all_gather(grad_attn_low, 'tensor', axis=0, tiled=True)]
    pallas_call x1 -> x2, Pallas kernels: 248 us -> 283 us  [the longest x1 203 us: weight_grads(): pl.pallas_call(grads_kernel, name='weight_grads', input_output_aliases={1...]
    dot_general x7 -> x4, matrix products: 41.9 us -> 16.8 us  [times_t(): lax.dot_general(left_mat, right_mat, (((1,), (1,)), ((), ())), preferred_...]
    dot_general x3 -> x0, matrix products: 22.8 us -> none  [the longest x1 8.52 us: body(): gate_acts = jnp.dot(hidden_all, w_gate, preferred_element_type=jnp.float32)]
    unnamed x83 -> x80, local copies, waits for them, and re-layouts: 17.9 us -> 16.9 us
  transfers between devices with their start and end apart: 8 -> 4, of which waited for: 7 -> 3; matrix products, arithmetic and copies ran while one was open for 4% -> 5% of each run, Pallas kernels for 37% -> 38%
where the time goes in v3:
time: 535 us; the launch traced here: 530 us
  Pallas kernels  283 us (53%)
  waiting for transfers between devices  74.4 us (14%)
  blocking collectives  56.2 us (11%)
  local copies, waits for them, and re-layouts  42.2 us (8%)
  matrix products  35.9 us (7%)
  other arithmetic  23.9 us (4%)
  between operations  14.5 us (3%)
    pallas_call x1, Pallas kernels, weight_grads(): pl.pallas_call(grads_kernel, name='weight_grads', input_output_aliases={1...  203 us
    pallas_call x1, Pallas kernels, mlp_both(): pl.pallas_call(mlp_kernel, name='feed_forward', out_shape=(shape((shard,...  79.5 us
    psum x1, blocking collectives, body(): gain_total = lax.psum(gain_stack, ('dp', 'tensor'))  43.9 us
    reduce_scatter x1, waiting for transfers between devices, body(): lax.psum_scatter(jnp.dot(mixed_low, w_out, preferred_element_type=jnp.flo...  32.4 us
    all_gather x1, waiting for transfers between devices, body(): gathered = lax.all_gather(tokens, 'tensor', axis=0, tiled=True)  22.7 us
    all_gather x1, waiting for transfers between devices, body(): attn_grad_all = lax.all_gather(grad_attn_low, 'tensor', axis=0, tiled=True)  18.5 us
    unnamed x80, local copies, waits for them, and re-layouts  16.9 us
    dot_general x4, matrix products, times_t(): lax.dot_general(left_mat, right_mat, (((1,), (1,)), ((), ())), preferred_...  16.8 us
  transfers between devices with their start and end apart: 4, of which 3 were waited for; matrix products, arithmetic and copies ran while one was open for 5% of the time, Pallas kernels for 38%

profile of v3, /device:TPU:0, one launch (start us, length us, event | category | flops | bytes accessed | tf_op | source)
XLA Modules:
  0.0 530.4 jit_solution(17806849757236838022)
XLA Ops:
  7.2 0.7 all-gather.3.cloned.1.call-update
  8.0 0.8 select_reduce_fusion.1
  8.8 0.7 select_reduce_fusion
  9.5 0.9 fusion.14
  10.4 1.8 broadcast_multiply_fusion
  12.2 22.7 %all-gather.3.cloned.1.call-done = bf16[512,2048]{1,0:T(8,128)(2,1)} async-done(((bf16[128,2048]{1,0:T(8,128)(2,1)}), bf16[512,2048]{1,0:T(8,128)(2,1)}) %all-gather.3.cloned.1.call-update) | async-done | bytes 2097168 | tf_op jit(solution)/shard_map/all_gather | solution.py:715
  34.9 3.9 multiply_reduce_fusion.4
  38.8 1.6 copy.54
  40.3 4.5 multiply_reduce_fusion.3
  44.8 6.0 %all-reduce.1 = (f32[512]{0:T(512)S(1)}, f32[512]{0:T(512)S(1)}) all-reduce(f32[512]{0:T(512)S(1)} %get-tuple-element.95, f32[512]{0:T(512)S(1)} %get-tuple-element.97), channel_id=1, replica_groups=mesh['dp'=8,'tensor'=4] {'tensor'}, use_global_device_ids=true, to_apply=%region_6.7 | all-reduce | flops 1024 | bytes 8192 | tf_op jit(solution)/shard_map/psum | solution.py:721
  50.9 1.1 multiply_multiply_fusion.1
  52.0 2.5 reshape.502
  54.5 3.6 fusion.23
  58.1 2.5 copy.57
  60.7 2.3 multiply_multiply_fusion
  63.0 2.6 reshape.503
  65.6 2.3 fusion.24
  67.9 0.5 fusion.15
  68.9 1.4 fusion.26
  70.3 0.6 fusion
  70.9 2.5 copy-done.22
  73.4 0.6 copy-done.36
  74.0 1.3 convolution_convert_fusion.2
  75.4 0.9 fusion.11
  76.3 0.8 copy-done.31
  77.1 2.6 convolution_convert_fusion
  80.0 32.4 %reduce-scatter.3.cloned.1.call-done = bf16[128,2048]{1,0:T(8,128)(2,1)} async-done(((bf16[512,2048]{1,0:T(8,128)(2,1)}), bf16[128,2048]{1,0:T(8,128)(2,1)}) %reduce-scatter.3.cloned.1.call-update) | async-done | bytes 524304 | tf_op jit(solution)/shard_map/reduce_scatter | solution.py:739
  112.4 2.1 convert_element_type.104.att_ref
  114.5 79.5 %feed_forward.1 = (bf16[128,2048]{1,0:T(8,128)(2,1)}, f32[128,2048]{1,0:T(8,128)}, bf16[128,2048]{1,0:T(8,128)(2,1)}, bf16[128,2048]{1,0:T(8,128)(2,1)}, f32[2,2...) custom-call(f32[128,2048]{1,0:T(8,128)} %convert_element_type.104.att_ref, ...), custom_call_target="tpu_custom_call" | custom-call | flops 25769803776 | bytes 41943040 | tf_op jit(solution)/shard_map/feed_forward/pallas_call | solution.py:648
  194.3 2.1 copy.89.mix_ref
  196.4 18.5 %all-gather.5.cloned.1.call-done = bf16[512,2048]{1,0:T(8,128)(2,1)} async-done(((bf16[128,2048]{1,0:T(8,128)(2,1)}), bf16[512,2048]{1,0:T(8,128)(2,1)}) %all-gather.5.cloned.1.call-update) | async-done | bytes 2097168 | tf_op jit(solution)/shard_map/all_gather | solution.py:813
  215.0 3.6 convolution_convert_fusion.1
  218.6 1.0 multiply_reduce_fusion
  219.6 1.2 multiply_convert_fusion
  220.9 0.8 fusion.6
  222.1 1.1 fusion.7
  223.1 1.6 fusion.8
  224.8 1.0 multiply_subtract_fusion
  226.1 0.7 copy.67
  227.2 0.6 copy-done.6
  228.1 0.7 copy.71
  229.8 6.3 %all-reduce = (f32[512]{0:T(512)S(1)}, f32[512]{0:T(512)S(1)}) all-reduce(f32[512]{0:T(512)S(1)} %get-tuple-element.56, f32[512]{0:T(512)S(1)} %get-tuple-element.58), channel_id=1, replica_groups=mesh['dp'=8,'tensor'=4] {'tensor'}, use_global_device_ids=true, to_apply=%region_12.13 | all-reduce | flops 1024 | bytes 8192 | tf_op jit(solution)/shard_map/psum | solution.py:824
  236.1 1.5 multiply_convert_fusion.2.dq_ref
  237.6 3.2 fusion.27
  241.1 1.3 copy-done.23
  242.4 3.3 fusion.28
  245.7 1.0 copy.90.dv_ref
  246.7 6.7 %add_convert_fusion = bf16[512,2048]{1,0:T(8,128)(2,1)} fusion(f32[512,2048]{1,0:T(8,128)} %fusion.27, f32[512,2048]{1,0:T(8,128)} %fusion.28, bf16[512,512]{0,1:T(8,128)(2,1)S(1)} %bitcast.115, bf16[2048,512]{1,0:T(8,128)(2,1)} %param.18), kind=kOutput, calls=%fused_computation.1 | convolution fusion | flops 1076887552 | bytes 13107200 | tf_op jit(solution)/shard_map/dot_general | solution.py:55
  253.4 203.3 %weight_grads.1 = (bf16[7,4,512,256]{3,2,1,0:T(8,128)(2,1)}, bf16[4,4,128,2048]{3,2,1,0:T(8,128)(2,1)}, bf16[4,4,128,2048]{3,2,1,0:T(8,128)(2,1)}) custom-call(bf16[128,2048]{1,0:T(8,128)(2,1)} %get-tuple-element.24.dml_ref, bf16[4,4,128,2048]{3,2,1,0:T(8,128)(2,1)} %get-tuple-element.25.gh_in, ...), custom_call_target="tpu_custom_call", output_to_operand_aliasing={{1}: (1, {}), {2}: (2, {})} | custom-call | flops 30064771072 | bytes 62914560 | tf_op jit(solution)/shard_map/weight_grads/pallas_call | solution.py:396
  456.7 3.0 convert_reduce_fusion
  459.8 1.2 slice_bitcast_fusion
  460.9 2.0 copy.74
  463.0 1.0 copy.75
  464.0 1.0 copy.76
  465.0 2.5 slice_convert_fusion
  467.5 2.8 fusion.22
  470.3 1.8 copy.77
  472.1 3.0 copy.78
  475.2 43.9 %psum.39 = f32[4,2048]{1,0:T(4,128)S(1)} all-reduce(f32[4,2048]{1,0:T(4,128)S(1)} %pad_maximum_fusion.8), channel_id=1, replica_groups=mesh['dp'=8,'tensor'=4] {'dp','tensor'}, use_global_device_ids=true, to_apply=%region_19.20 | all-reduce | flops 8192 | bytes 65536 | tf_op jit(solution)/shard_map/psum | solution.py:852
  519.1 0.6 fusion.25
  519.7 0.6 constant_dynamic-slice_fusion.1
  520.3 0.6 constant_dynamic-slice_fusion
  520.9 2.0 add_convert_fusion.1
  522.9 0.8 copy.132
  (93 shorter events, 3.9 us)
Async XLA Ops:
  7.2 27.7 %copy-start = (bf16[2048,512]{1,0:T(8,128)(2,1)S(1)}, bf16[2048,512]{1,0:T(8,128)(2,1)}, u32[]{:S(2)}) copy-start(bf16[2048,512]{1,0:T(8,128)(2,1)} %param.16) | copy-start | bytes 6291460
  7.2 27.7 %all-gather.3.cloned.1.call-start = ((), (), s32[]{:S(2)}) async-start(), calls=%async_computation.2 | async-start | bytes 2621440 | tf_op jit(solution)/shard_map/all_gather | solution.py:715
  7.9 104.5 %reduce-scatter.3.cloned.1.call-start = ((), (), s32[]{:S(2)}) async-start(), calls=%async_computation.3 | async-start | bytes 2621440 | tf_op jit(solution)/shard_map/reduce_scatter | solution.py:739
  40.3 10.6 %copy-start.32 = (f32[512]{0:T(512)S(1)}, f32[512]{0:T(512)}, u32[]{:S(2)}) copy-start(f32[512]{0:T(512)} %param.23) | copy-start | bytes 6148
  58.1 2.5 copy-start.33
  65.6 2.3 copy-start.18
  65.6 2.3 copy-start.19
  65.6 2.3 copy-start.27
  67.9 1.0 copy-start.24
  68.5 1.8 copy-start.10
  68.5 1.8 copy-start.12
  68.5 1.8 copy-start.14
  68.5 1.8 copy-start.16
  70.3 5.1 copy-start.2
  70.3 3.1 copy-start.22
  70.3 3.7 copy-start.36
  75.3 1.0 copy-start.28
  75.4 1.8 copy-start.35
  76.3 0.8 copy-start.31
  79.8 135.2 %all-gather.5.cloned.1.call-start = ((), (), s32[]{:S(2)}) async-start(), calls=%async_computation.4 | async-start | bytes 2621440 | tf_op jit(solution)/shard_map/all_gather | solution.py:813
  194.1 326.8 %reduce-scatter.5.cloned.1.call-start = ((), (), s32[]{:S(2)}) async-start(), calls=%async_computation.5 | async-start | bytes 2621440 | tf_op jit(solution)/shard_map/reduce_scatter | solution.py:836
  215.0 3.7 copy-start.3
  215.0 3.7 copy-start.29
  219.6 1.2 copy-start.15
  219.6 1.2 copy-start.17
  220.9 1.0 copy-start.11
  220.9 1.2 copy-start.13
  223.1 1.7 copy-start.26
  226.8 1.0 copy-start.6
  227.8 1.2 copy-start.4
  228.8 1.0 copy-start.7
  237.5 3.3 copy-start.20
  237.5 3.3 copy-start.5
  237.5 3.3 copy-start.8
  240.8 1.6 copy-start.23
  242.4 3.3 copy-start.21
  242.4 3.3 copy-start.9
  472.1 3.1 copy-start.34
  472.1 48.8 %copy-start.25 = (f32[128,2048]{1,0:T(8,128)S(1)}, f32[128,2048]{1,0:T(8,128)}, u32[]{:S(2)}) copy-start(f32[128,2048]{1,0:T(8,128)} %get-tuple-element.22) | copy-start | bytes 3145732
  472.1 51.6 %copy-start.1 = (bf16[2048,512]{1,0:T(8,128)(2,1)S(1)}, bf16[2048,512]{1,0:T(8,128)(2,1)}, u32[]{:S(2)}) copy-start(bf16[2048,512]{1,0:T(8,128)(2,1)} %param.16) | copy-start | bytes 6291460
  520.9 2.0 copy-start.30
Sparse Core Ops, SparseCore 0:
  9.6 25.2 all-gather.2
  79.9 32.4 reduce-scatter.2
  194.2 20.7 all-gather.4
  253.5 43.8 reduce-scatter.4
